TPU v7x, 32 devices: a whole 2x2x4 slice. The times are simulated.
32 devices in a mesh: ctx: 16 (over z, x, core), fsdp: 2 (over y).
Axes of the slice: x: 2, y: 2, z: 4, core: 2. Of those that a mesh axis runs over, the one named last changes fastest.
Arguments:
- hidden_in: bfloat16 [2, 2048, 1024], P('fsdp', 'ctx'), may hold values from -6 to 6
- out_grad: bfloat16 [2, 2048, 1024], P('fsdp', 'ctx'), may hold values from -6 to 6
- doc_lengths: int32 [2, 16], P('fsdp'), may hold values from 1 to 512, 2048 in all within a row
- block_order: int32 [2, 32], P('fsdp'), may hold values from 0 to 31, as said below
- routes: int32 [2, 2048, 8], P('fsdp', 'ctx'), may hold values from 0 to 15, all different within a row
- attn_norm: bfloat16 [1024], P(('ctx', 'fsdp')), may hold values from 0.5 to 1.5
- w_query: bfloat16 [1024, 1024], P(('ctx', 'fsdp')), may hold values from -0.625 to 0.625
- w_key: bfloat16 [1024, 512], P(('ctx', 'fsdp')), may hold values from -0.625 to 0.625
- w_value: bfloat16 [1024, 512], P(('ctx', 'fsdp')), may hold values from -0.1875 to 0.1875
- w_output: bfloat16 [1024, 1024], P(('ctx', 'fsdp')), may hold values from -3 to 3
- ffn_norm: bfloat16 [1024], P(('ctx', 'fsdp')), may hold values from 0.5 to 1.5
- w_router: bfloat16 [1024, 16], P(('ctx', 'fsdp')), may hold values from -0.09375 to 0.09375
- w_gate_up: bfloat16 [1024, 16384], P(('ctx', 'fsdp')), may hold values from -0.1875 to 0.1875
- w_down: bfloat16 [1024, 8192], P(('ctx', 'fsdp')), may hold values from -4 to 4
Outputs:
- hidden_out: bfloat16 [2, 2048, 1024], P('fsdp', 'ctx')
- grad_in: float32 [2, 2048, 1024], P('fsdp', 'ctx')
- grad_attn_norm: float32 [1024], P(('ctx', 'fsdp'))
- grad_query: float32 [1024, 1024], P(('ctx', 'fsdp'))
- grad_key: float32 [1024, 512], P(('ctx', 'fsdp'))
- grad_value: float32 [1024, 512], P(('ctx', 'fsdp'))
- grad_output: float32 [1024, 1024], P(('ctx', 'fsdp'))
- grad_ffn_norm: float32 [1024], P(('ctx', 'fsdp'))
- grad_router: float32 [1024, 16], P(('ctx', 'fsdp'))
- grad_gate_up: float32 [1024, 16384], P(('ctx', 'fsdp'))
- grad_down: float32 [1024, 8192], P(('ctx', 'fsdp'))
Inputs may be any that keep to these rules, and one draw needn't show every extreme that they name: `block_order`: in each sequence, storage blocks 2 c and 2 c + 1 (those of ctx index c) hold the sequence blocks p and 31 - p, in either order; every sequence block is held once. `doc_lengths`: each row sums to 2048; the longest document has exactly 512 tokens. `routes`: each token names 8 different experts; every expert is named by some token.
All inputs are finite; a program needn't handle non-finite values.
Results may differ from a plain program's by a relative error of at most 0.017.
Values may be sent and summed in bfloat16 or wider, within the bound.
No kernel may reach another device: no remote copies, remote signals or barrier semaphores. Data moves between devices by JAX's collectives and lax.ppermute only.
A program may use at most 320 MiB of HBM per device.

v0:
```python
import jax
import jax.numpy as jnp
from jax import lax
from jax.sharding import PartitionSpec as P

D = 1024
H = 16
KVH = 8
HD = 64
F = 512
E = 16


EPSILON = 1e-06
SCORE_SCALE = 0.015625
RESIDUAL_SCALE = 0.22
THETA = 10000.0
NEGATIVE = -1e30
HIGHEST = lax.Precision.HIGHEST


def norm_forward(values, gain_vec):
    factor = lax.rsqrt(jnp.mean(values * values, axis=-1, keepdims=True) + EPSILON)
    return (values * factor * gain_vec, factor)


def norm_backward(values, factor, gain_vec, upstream):
    scaled = values * factor
    inner_vec = upstream * gain_vec
    grad_values = factor * (
        inner_vec - scaled * jnp.mean(inner_vec * scaled, axis=-1, keepdims=True)
    )
    return (grad_values, jnp.sum(upstream * scaled, axis=0))


def rope_tables(places, head_width):
    half_width = head_width // 2
    frequency = THETA ** (-jnp.arange(half_width, dtype=jnp.float32) / half_width)
    angles = places.astype(jnp.float32)[:, None] * frequency[None, :]
    return (jnp.cos(angles)[:, None, :], jnp.sin(angles)[:, None, :])


def rotate(values, cosine, sine, sign_val):
    half_width = values.shape[-1] // 2
    first_half = values[..., :half_width]
    second_half = values[..., half_width:]
    return jnp.concatenate(
        [
            first_half * cosine - sign_val * second_half * sine,
            second_half * cosine + sign_val * first_half * sine,
        ],
        axis=-1,
    )


def block_scores(query_grp, keys_blk, key_places, own_places, own_start):
    raw_scores = jnp.einsum(
        "qhgd,khd->hgqk", query_grp, keys_blk, preferred_element_type=jnp.float32
    )
    visible = (key_places[None, :] <= own_places[:, None]) & (
        key_places[None, :] >= own_start[:, None]
    )
    return (jnp.where(visible[None, None], raw_scores * SCORE_SCALE, NEGATIVE), visible)


def per_device(
    hidden_in,
    out_grad,
    doc_lengths,
    block_order,
    routes,
    attn_norm,
    w_query,
    w_key,
    w_value,
    w_output,
    ffn_norm,
    w_router,
    w_gate_up,
    w_down,
):
    ctx_count = lax.axis_size("ctx")
    ctx_place = lax.axis_index("ctx")
    tok_count = hidden_in.shape[1]
    seq_len = tok_count * ctx_count
    block_len = tok_count // 2
    key_len = min(1024, seq_len)
    block_count = seq_len // key_len
    groups = H // KVH
    kv_width = KVH * HD
    block_ids = block_order[0]
    places_all = (
        block_ids[:, None] * block_len + jnp.arange(block_len, dtype=jnp.int32)[None, :]
    ).reshape(seq_len)
    own_places = lax.dynamic_slice_in_dim(places_all, ctx_place * tok_count, tok_count)
    lengths = doc_lengths[0]
    doc_first = jnp.cumsum(lengths) - lengths
    own_start = jnp.max(
        jnp.where(doc_first[None, :] <= own_places[:, None], doc_first[None, :], 0), axis=1
    )
    gain_one, query_full, key_full, value_full, output_full, gain_two, router_full = (
        lax.all_gather(attn_norm, ("ctx", "fsdp"), axis=0, tiled=True),
        lax.all_gather(w_query, ("ctx", "fsdp"), axis=0, tiled=True),
        lax.all_gather(w_key, ("ctx", "fsdp"), axis=0, tiled=True),
        lax.all_gather(w_value, ("ctx", "fsdp"), axis=0, tiled=True),
        lax.all_gather(w_output, ("ctx", "fsdp"), axis=0, tiled=True),
        lax.all_gather(ffn_norm, ("ctx", "fsdp"), axis=0, tiled=True),
        lax.all_gather(w_router, ("ctx", "fsdp"), axis=0, tiled=True),
    )
    gain_one = gain_one.astype(jnp.float32)
    gain_two = gain_two.astype(jnp.float32)
    hidden = hidden_in[0].astype(jnp.float32)
    normed_f, factor_one = norm_forward(hidden, gain_one)
    normed = normed_f.astype(jnp.bfloat16)
    cosine, sine = rope_tables(own_places, HD)
    query_pre = jnp.dot(normed, query_full, preferred_element_type=jnp.float32).reshape(
        tok_count, H, HD
    )
    queries = rotate(query_pre, cosine, sine, 1.0).astype(jnp.bfloat16)
    key_pre = jnp.dot(normed, key_full, preferred_element_type=jnp.float32).reshape(
        tok_count, KVH, HD
    )
    keys = rotate(key_pre, cosine, sine, 1.0).astype(jnp.bfloat16).reshape(tok_count, kv_width)
    values = jnp.dot(normed, value_full, preferred_element_type=jnp.float32).astype(jnp.bfloat16)
    keys_all, values_all = (
        lax.all_gather(keys, "ctx", axis=0, tiled=True),
        lax.all_gather(values, "ctx", axis=0, tiled=True),
    )
    query_grp = queries.reshape(tok_count, KVH, groups, HD)
    places_blocks = places_all.reshape(block_count, key_len)

    def stat_step(running, block_item):
        row_top, row_total = running
        keys_blk, key_places = block_item
        scores, visible = block_scores(query_grp, keys_blk, key_places, own_places, own_start)
        new_top = jnp.maximum(row_top, jnp.max(scores, axis=-1))
        shifted = jnp.where(visible[None, None], jnp.exp(scores - new_top[..., None]), 0.0)
        return ((new_top, row_total * jnp.exp(row_top - new_top) + jnp.sum(shifted, axis=-1)), None)

    stat_init = (
        jnp.full((KVH, groups, tok_count), NEGATIVE, jnp.float32),
        jnp.zeros((KVH, groups, tok_count), jnp.float32),
    )
    keys_blocks = keys_all.reshape(block_count, key_len, KVH, HD)
    values_blocks = values_all.reshape(block_count, key_len, KVH, HD)
    (row_top, row_total), ignored = lax.scan(stat_step, stat_init, (keys_blocks, places_blocks))
    log_total = row_top + jnp.log(row_total)

    def value_step(running, block_item):
        keys_blk, values_blk, key_places = block_item
        scores, visible = block_scores(query_grp, keys_blk, key_places, own_places, own_start)
        attn_weights = jnp.exp(scores - log_total[..., None]).astype(jnp.bfloat16)
        return (
            running
            + jnp.einsum(
                "hgqk,khd->qhgd", attn_weights, values_blk, preferred_element_type=jnp.float32
            ),
            None,
        )

    attended_f, ignored = lax.scan(
        value_step,
        jnp.zeros((tok_count, KVH, groups, HD), jnp.float32),
        (keys_blocks, values_blocks, places_blocks),
    )
    attended = attended_f.reshape(tok_count, H * HD).astype(jnp.bfloat16)
    middle = hidden + RESIDUAL_SCALE * jnp.dot(
        attended, output_full, preferred_element_type=jnp.float32
    )
    mixed_f, factor_two = norm_forward(middle, gain_two)
    mixed_in = mixed_f.astype(jnp.bfloat16)
    logits = jnp.dot(mixed_in, router_full, preferred_element_type=jnp.float32)
    onehot = (routes[0][:, :, None] == jnp.arange(E, dtype=jnp.int32)[None, None, :]).astype(
        jnp.float32
    )
    chosen = jnp.einsum("tke,te->tk", onehot, logits, precision=HIGHEST)
    gate_probs = jax.nn.softmax(chosen, axis=-1)
    combine = jnp.einsum("tk,tke->te", gate_probs, onehot, precision=HIGHEST)
    grad_top = out_grad[0].astype(jnp.float32)
    gate_whole, down_whole = (
        lax.all_gather(w_gate_up, ("ctx", "fsdp"), axis=0, tiled=True),
        lax.all_gather(w_down, ("ctx", "fsdp"), axis=0, tiled=True),
    )
    gate_up_w = gate_whole.reshape(D, E, 2, F)
    down_w = down_whole.reshape(D, E, F)
    gate_up_val = jnp.einsum(
        "td,degu->tegu", mixed_in, gate_up_w, preferred_element_type=jnp.float32
    )
    gate_part = gate_up_val[:, :, 0, :]
    up_part = gate_up_val[:, :, 1, :]
    silu_gate = jax.nn.silu(gate_part)
    activation = (silu_gate * up_part).astype(jnp.bfloat16)
    expert_out = jnp.einsum("teu,deu->ted", activation, down_w, preferred_element_type=jnp.float32)
    moe_part = jnp.einsum("te,ted->td", combine, expert_out, precision=HIGHEST)
    hidden_out = (middle + RESIDUAL_SCALE * moe_part).astype(jnp.bfloat16)
    grad_moe = RESIDUAL_SCALE * grad_top
    grad_expert = (combine[:, :, None] * grad_moe[:, None, :]).astype(jnp.bfloat16)
    grad_combine_part = jnp.einsum("ted,td->te", expert_out, grad_moe, precision=HIGHEST)
    grad_down = jnp.einsum(
        "teu,ted->deu", activation, grad_expert, preferred_element_type=jnp.float32
    )
    grad_act = jnp.einsum("ted,deu->teu", grad_expert, down_w, preferred_element_type=jnp.float32)
    sigmoid_g = jax.nn.sigmoid(gate_part)
    grad_both = jnp.stack(
        [
            grad_act * up_part * sigmoid_g * (1.0 + gate_part * (1.0 - sigmoid_g)),
            grad_act * silu_gate,
        ],
        axis=2,
    ).astype(jnp.bfloat16)
    grad_gate_up = jnp.einsum(
        "td,tegu->degu", mixed_in, grad_both, preferred_element_type=jnp.float32
    )
    grad_mixed_part = jnp.einsum(
        "tegu,degu->td", grad_both, gate_up_w, preferred_element_type=jnp.float32
    )
    share_gate_up, share_down = (
        lax.psum_scatter(
            grad_gate_up.reshape(D, E * 2 * F), ("ctx", "fsdp"), scatter_dimension=0, tiled=True
        ),
        lax.psum_scatter(
            grad_down.reshape(D, E * F), ("ctx", "fsdp"), scatter_dimension=0, tiled=True
        ),
    )
    grad_gates = jnp.einsum("te,tke->tk", grad_combine_part, onehot, precision=HIGHEST)
    grad_chosen = gate_probs * (
        grad_gates - jnp.sum(gate_probs * grad_gates, axis=-1, keepdims=True)
    )
    grad_logits = jnp.einsum("tk,tke->te", grad_chosen, onehot, precision=HIGHEST).astype(
        jnp.bfloat16
    )
    grad_router = jnp.einsum("td,te->de", mixed_in, grad_logits, preferred_element_type=jnp.float32)
    grad_mixed = grad_mixed_part + jnp.einsum(
        "te,de->td", grad_logits, router_full, preferred_element_type=jnp.float32
    )
    grad_middle_norm, grad_gain_two = norm_backward(middle, factor_two, gain_two, grad_mixed)
    grad_middle = grad_top + grad_middle_norm
    grad_attn = (RESIDUAL_SCALE * grad_middle).astype(jnp.bfloat16)
    grad_output = jnp.einsum("tc,td->cd", attended, grad_attn, preferred_element_type=jnp.float32)
    grad_attended = jnp.einsum(
        "td,cd->tc", grad_attn, output_full, preferred_element_type=jnp.float32
    ).astype(jnp.bfloat16)
    grad_attended_grp = grad_attended.reshape(tok_count, KVH, groups, HD)
    row_delta = jnp.einsum(
        "qhgd,qhgd->hgq", grad_attended_grp.astype(jnp.float32), attended_f, precision=HIGHEST
    )

    def back_step(running, block_item):
        keys_blk, values_blk, key_places = block_item
        scores, visible = block_scores(query_grp, keys_blk, key_places, own_places, own_start)
        attn_weights = jnp.exp(scores - log_total[..., None])
        grad_weights = jnp.einsum(
            "qhgd,khd->hgqk", grad_attended_grp, values_blk, preferred_element_type=jnp.float32
        )
        grad_raw = (attn_weights * (grad_weights - row_delta[..., None]) * SCORE_SCALE).astype(
            jnp.bfloat16
        )
        running = running + jnp.einsum(
            "hgqk,khd->qhgd", grad_raw, keys_blk, preferred_element_type=jnp.float32
        )
        grad_keys = jnp.einsum(
            "hgqk,qhgd->khd", grad_raw, query_grp, preferred_element_type=jnp.float32
        ).reshape(key_len, kv_width)
        grad_values = jnp.einsum(
            "hgqk,qhgd->khd",
            attn_weights.astype(jnp.bfloat16),
            grad_attended_grp,
            preferred_element_type=jnp.float32,
        ).reshape(key_len, kv_width)
        return (running, (grad_keys, grad_values))

    grad_queries, (keys_terms, values_terms) = lax.scan(
        back_step,
        jnp.zeros((tok_count, KVH, groups, HD), jnp.float32),
        (keys_blocks, values_blocks, places_blocks),
    )
    grad_keys_own, grad_values_own = (
        lax.psum_scatter(
            keys_terms.reshape(seq_len, kv_width), "ctx", scatter_dimension=0, tiled=True
        ),
        lax.psum_scatter(
            values_terms.reshape(seq_len, kv_width), "ctx", scatter_dimension=0, tiled=True
        ),
    )
    grad_query_pre = (
        rotate(grad_queries.reshape(tok_count, H, HD), cosine, sine, -1.0)
        .reshape(tok_count, H * HD)
        .astype(jnp.bfloat16)
    )
    grad_key_pre = (
        rotate(grad_keys_own.reshape(tok_count, KVH, HD), cosine, sine, -1.0)
        .reshape(tok_count, kv_width)
        .astype(jnp.bfloat16)
    )
    grad_value_pre = grad_values_own.astype(jnp.bfloat16)
    grad_query = jnp.einsum("td,tc->dc", normed, grad_query_pre, preferred_element_type=jnp.float32)
    grad_key = jnp.einsum("td,tc->dc", normed, grad_key_pre, preferred_element_type=jnp.float32)
    grad_value = jnp.einsum("td,tc->dc", normed, grad_value_pre, preferred_element_type=jnp.float32)
    grad_normed = jnp.einsum(
        "tc,dc->td", grad_query_pre, query_full, preferred_element_type=jnp.float32
    )
    grad_normed = grad_normed + jnp.einsum(
        "tc,dc->td", grad_key_pre, key_full, preferred_element_type=jnp.float32
    )
    grad_normed = grad_normed + jnp.einsum(
        "tc,dc->td", grad_value_pre, value_full, preferred_element_type=jnp.float32
    )
    grad_hidden_norm, grad_gain_one = norm_backward(hidden, factor_one, gain_one, grad_normed)
    grad_in = grad_middle + grad_hidden_norm
    (
        share_gain_one,
        share_query,
        share_key,
        share_value,
        share_output,
        share_gain_two,
        share_router,
    ) = (
        lax.psum_scatter(grad_gain_one, ("ctx", "fsdp"), scatter_dimension=0, tiled=True),
        lax.psum_scatter(grad_query, ("ctx", "fsdp"), scatter_dimension=0, tiled=True),
        lax.psum_scatter(grad_key, ("ctx", "fsdp"), scatter_dimension=0, tiled=True),
        lax.psum_scatter(grad_value, ("ctx", "fsdp"), scatter_dimension=0, tiled=True),
        lax.psum_scatter(grad_output, ("ctx", "fsdp"), scatter_dimension=0, tiled=True),
        lax.psum_scatter(grad_gain_two, ("ctx", "fsdp"), scatter_dimension=0, tiled=True),
        lax.psum_scatter(grad_router, ("ctx", "fsdp"), scatter_dimension=0, tiled=True),
    )
    return (
        hidden_out[None],
        grad_in[None],
        share_gain_one,
        share_query,
        share_key,
        share_value,
        share_output,
        share_gain_two,
        share_router,
        share_gate_up,
        share_down,
    )


def solution(mesh):
    return jax.shard_map(
        per_device,
        mesh=mesh,
        in_specs=(
            P("fsdp", "ctx", None),
            P("fsdp", "ctx", None),
            P("fsdp", None),
            P("fsdp", None),
            P("fsdp", "ctx", None),
            P(("ctx", "fsdp")),
            P(("ctx", "fsdp"), None),
            P(("ctx", "fsdp"), None),
            P(("ctx", "fsdp"), None),
            P(("ctx", "fsdp"), None),
            P(("ctx", "fsdp")),
            P(("ctx", "fsdp"), None),
            P(("ctx", "fsdp"), None),
            P(("ctx", "fsdp"), None),
        ),
        out_specs=(
            P("fsdp", "ctx", None),
            P("fsdp", "ctx", None),
            P(("ctx", "fsdp")),
            P(("ctx", "fsdp"), None),
            P(("ctx", "fsdp"), None),
            P(("ctx", "fsdp"), None),
            P(("ctx", "fsdp"), None),
            P(("ctx", "fsdp")),
            P(("ctx", "fsdp"), None),
            P(("ctx", "fsdp"), None),
            P(("ctx", "fsdp"), None),
        ),
        check_vma=False,
    )
```

profile of v0, /device:TPU:0, one launch (start us, length us, event | category | flops | bytes accessed | tf_op | source)
XLA Modules:
  0.0 3783.1 jit_solution(14399923190856398702)
XLA Ops:
  11.2 42.0 %all-reduce.5 = (bf16[1024]{0:T(1024)(128)(2,1)S(1)}, bf16[1024]{0:T(1024)(128)(2,1)S(1)}) all-reduce(bf16[1024]{0:T(1024)(128)(2,1)S(1)} %dynamic-update-slice, bf16[1024]{0:T(1024)(128)(2,1)S(1)} %dynamic-update-slice.1), channel_id=1, replica_groups=mesh['ctx'=16,'fsdp'=2] {'ctx','fsdp'}, use_global_device_ids=true, to_apply=%add | all-reduce | flops 2048 | bytes 8192
  56.0 11.4 all-gather.14.cloned.1.call-done
  71.2 51.8 %all-gather.10.cloned.1.call-done = bf16[1024,512]{1,0:T(8,128)(2,1)} async-done(((bf16[32,512]{1,0:T(8,128)(2,1)}), bf16[1024,512]{1,0:T(8,128)(2,1)}) %all-gather.10.cloned.1.call-update) | async-done | bytes 1048592 | tf_op jit(solution)/shard_map/all_gather | solution.py:105
  123.0 2.2 convolution_convert_fusion.1
  128.1 67.6 %all-gather = bf16[32,32,16]{1,2,0:T(8,128)(2,1)S(1)} all-gather(bf16[1,32,16]{1,2,0:T(8,128)(2,1)S(1)} %bitcast.404), channel_id=1, replica_groups=mesh['ctx'=16,'fsdp'=2] {'ctx','fsdp'}, dimensions={0}, use_global_device_ids=true | all-gather | bytes 33792 | tf_op jit(solution)/shard_map/all_gather | solution.py:108
  197.2 2.9 copy.108
  201.0 23.6 all-gather.16.cloned.1.call-done
  224.6 4.5 reshape.439
  229.0 2.2 copy.111
  231.3 36.2 all-gather.12.cloned.1.call-done
  267.5 6.2 reshape.484
  273.7 5.5 copy.110
  279.2 7.5 while.39
  280.9 2.0 select_reduce_fusion.5
  284.6 2.0 select_reduce_fusion.5
  286.7 8.6 while.40
  286.9 4.1 fusion.211
  291.2 4.1 fusion.211
  297.8 28.0 all-gather.20.cloned.1.call-done
  325.8 2.2 multiply_reduce_fusion.2
  329.4 113.0 %all-gather.24.cloned.1.call-done = bf16[1024,8192]{1,0:T(8,128)(2,1)} async-done(((bf16[32,8192]{1,0:T(8,128)(2,1)}), bf16[1024,8192]{1,0:T(8,128)(2,1)}) %all-gather.24.cloned.1.call-update) | async-done | bytes 16777232 | tf_op jit(solution)/shard_map/all_gather | solution.py:182
  442.4 22.6 copy.117
  465.0 173.5 %all-gather.22.cloned.1.call-done = bf16[1024,16384]{1,0:T(8,128)(2,1)} async-done(((bf16[32,16384]{1,0:T(8,128)(2,1)}), bf16[1024,16384]{1,0:T(8,128)(2,1)}) %all-gather.22.cloned.1.call-update) | async-done | bytes 33554448 | tf_op jit(solution)/shard_map/all_gather | solution.py:181
  638.6 44.0 %copy.114 = bf16[1024,16384]{0,1:T(8,128)(2,1)} copy(bf16[1024,16384]{1,0:T(8,128)(2,1)} %all-gather.22.cloned.1.call-done) | data formatting | bytes 67108864 | tf_op jit(solution)/shard_map/all_gather | solution.py:181
  682.6 19.2 fusion.106
  701.8 4.8 multiply_convert_fusion.3
  706.7 9.1 convolution_bitcast_fusion.1
  715.8 14.7 fusion.78
  732.5 13.0 fusion.73
  745.5 14.2 fusion.75
  761.5 12.7 fusion.55
  776.8 1.8 copy.122
  779.9 48.2 %while.41 = (s32[]{:T(128)}, f32[128,8,2,64]{0,3,2,1:T(8,128)S(1)}, f32[2,1024,512]{2,1,0:T(8,128)}, f32[2,1024,512]{2,1,0:T(8,128)}, bf16[2,1024,8,64]{1,3,2,0:...) while((s32[]{:T(128)}, f32[128,8,2,64]{0,3,2,1:T(8,128)S(1)}, ...), condition=%wide.region_15.16_spmd.clone, body=%wide.region_14.15_spmd.clone.sunk | while | flops 1365901312 | bytes 107386168 | solution.py:272
  781.7 3.4 fusion.225
  785.1 4.5 fusion.223
  789.6 3.0 copy.220
  792.6 3.2 fusion.224
  797.4 1.9 copy.221
  799.3 4.8 constant_dynamic-update-slice_fusion.3
  805.7 3.4 fusion.225
  809.1 4.5 fusion.223
  813.6 3.0 copy.220
  816.6 3.2 fusion.224
  821.4 1.9 copy.221
  823.3 4.8 constant_dynamic-update-slice_fusion.3
  830.2 2.8 fusion.118
  833.2 2.8 fusion.114
  836.1 62.9 %reduce-scatter.14.cloned.1.call-done = f32[128,512]{1,0:T(8,128)} async-done(((f32[2048,512]{1,0:T(8,128)}), f32[128,512]{1,0:T(8,128)}) %reduce-scatter.14.cloned.1.call-update) | async-done | bytes 262160 | tf_op jit(solution)/shard_map/reduce_scatter | solution.py:281
  899.0 2.8 fusion.120
  901.9 73.0 %reduce-scatter.12.cloned.1.call-done = f32[128,512]{1,0:T(8,128)} async-done(((f32[2048,512]{1,0:T(8,128)}), f32[128,512]{1,0:T(8,128)}) %reduce-scatter.12.cloned.1.call-update) | async-done | bytes 262160 | tf_op jit(solution)/shard_map/reduce_scatter | solution.py:278
  977.8 1.9 fusion.112
  979.8 13.5 fusion.57
  993.3 31.1 copy.131
  1026.0 24.8 fusion.68
  1050.9 65.9 %copy.129 = f32[1024,16384]{1,0:T(8,128)} copy(f32[1024,16384]{0,1:T(8,128)} %bitcast.55) | data formatting | bytes 134217728 | tf_op jit(solution)/shard_map/reshape | solution.py:219
  1121.3 1.8 convolution_add_fusion.1
  1123.2 1.9 fusion.93
  1125.1 40.4 %all-reduce.4 = (f32[1024]{0:T(1024)S(1)}, f32[1024]{0:T(1024)S(1)}) all-reduce(f32[1024]{0:T(1024)S(1)} %get-tuple-element.389, f32[1024]{0:T(1024)S(1)} %copy-done.44), channel_id=4, replica_groups=mesh['ctx'=16,'fsdp'=2] {'ctx','fsdp'}, use_global_device_ids=true, to_apply=%region_20.21.clone | all-reduce | flops 2048 | bytes 16384
  1167.7 83.0 %reduce-scatter.22.cloned.1.call-done = f32[32,1024]{1,0:T(8,128)} async-done(((f32[1024,1024]{1,0:T(8,128)}), f32[32,1024]{1,0:T(8,128)}) %reduce-scatter.22.cloned.1.call-update) | async-done | bytes 131088 | tf_op jit(solution)/shard_map/reduce_scatter | solution.py:323
  1250.7 141.3 %reduce-scatter.16.cloned.1.call-done = f32[32,1024]{1,0:T(8,128)} async-done(((f32[1024,1024]{1,0:T(8,128)}), f32[32,1024]{1,0:T(8,128)}) %reduce-scatter.16.cloned.1.call-update) | async-done | bytes 131088 | tf_op jit(solution)/shard_map/reduce_scatter | solution.py:320
  1392.0 136.2 %reduce-scatter.20.cloned.1.call-done = f32[32,512]{1,0:T(8,128)} async-done(((f32[1024,512]{1,0:T(8,128)}), f32[32,512]{1,0:T(8,128)}) %reduce-scatter.20.cloned.1.call-update) | async-done | bytes 65552 | tf_op jit(solution)/shard_map/reduce_scatter | solution.py:322
  1528.2 136.0 %reduce-scatter.18.cloned.1.call-done = f32[32,512]{1,0:T(8,128)} async-done(((f32[1024,512]{1,0:T(8,128)}), f32[32,512]{1,0:T(8,128)}) %reduce-scatter.18.cloned.1.call-update) | async-done | bytes 65552 | tf_op jit(solution)/shard_map/reduce_scatter | solution.py:321
  1664.1 705.2 %reduce-scatter.26.cloned.1.call-done = f32[32,8192]{1,0:T(8,128)} async-done(((f32[1024,8192]{1,0:T(8,128)}), f32[32,8192]{1,0:T(8,128)}) %reduce-scatter.26.cloned.1.call-update) | async-done | bytes 1048592 | tf_op jit(solution)/shard_map/reduce_scatter | solution.py:221
  2369.3 1406.8 %reduce-scatter.24.cloned.1.call-done = f32[32,16384]{1,0:T(8,128)} async-done(((f32[1024,16384]{1,0:T(8,128)}), f32[32,16384]{1,0:T(8,128)}) %reduce-scatter.24.cloned.1.call-update) | async-done | bytes 2097168 | tf_op jit(solution)/shard_map/reduce_scatter | solution.py:218
  (250 shorter events, 50.5 us)
Async XLA Ops:
  7.2 115.8 %copy-start.7 = (bf16[1,128,1024]{2,1,0:T(8,128)(2,1)S(1)}, bf16[1,128,1024]{2,1,0:T(8,128)(2,1)}, u32[]{:S(2)}) copy-start(bf16[1,128,1024]{2,1,0:T(8,128)(2,1)} %param.20) | copy-start | bytes 786436
  7.2 120.3 %copy-start.51 = (s32[1,16]{1,0:T(1,128)S(1)}, s32[1,16]{1,0:T(1,128)}, u32[]{:S(2)}) copy-start(s32[1,16]{1,0:T(1,128)} %param.22) | copy-start | bytes 196
  7.2 120.8 %copy-start.49 = (s32[1,128,8]{1,2,0:T(8,128)S(1)}, s32[1,128,8]{1,2,0:T(8,128)}, u32[]{:S(2)}) copy-start(s32[1,128,8]{1,2,0:T(8,128)} %param.24) | copy-start | bytes 12292
  7.2 60.2 %all-gather.14.cloned.1.call-start = ((), (), s32[]{:S(2)}) async-start(), calls=%async_computation.11 | async-start | bytes 1081344 | tf_op jit(solution)/shard_map/all_gather | solution.py:104
  7.9 115.1 %all-gather.10.cloned.1.call-start = ((), (), s32[]{:S(2)}) async-start(), calls=%async_computation.9 | async-start | bytes 1081344 | tf_op jit(solution)/shard_map/all_gather | solution.py:105
  8.7 119.4 %copy-start.50 = (bf16[32,16]{0,1:T(8,128)(2,1)S(1)}, bf16[32,16]{0,1:T(8,128)(2,1)}, u32[]{:S(2)}) copy-start(bf16[32,16]{0,1:T(8,128)(2,1)} %param.31) | copy-start | bytes 3076
  8.7 188.5 %all-gather.18.cloned.1.call-start = ((), (), s32[]{:S(2)}) async-start(), calls=%async_computation.13 | async-start | bytes 2162688 | tf_op jit(solution)/shard_map/all_gather | solution.py:103
  9.4 215.1 %all-gather.16.cloned.1.call-start = ((), (), s32[]{:S(2)}) async-start(), calls=%async_computation.12 | async-start | bytes 2228224 | tf_op jit(solution)/shard_map/all_gather | solution.py:126
  53.2 146.8 %copy-start.31 = (f32[1024]{0:T(1024)}, f32[1024]{0:T(1024)S(1)}, u32[]{:S(2)}) copy-start(f32[1024]{0:T(1024)S(1)} %convert_element_type.122) | copy-start | bytes 12292
  55.3 144.8 %copy-start.42 = (f32[128]{0:T(128)}, f32[128]{0:T(128)S(1)}, u32[]{:S(2)}) copy-start(f32[128]{0:T(128)S(1)} %add_rsqrt_fusion.1) | copy-start | bytes 1540
  56.0 144.9 %copy-start.29 = (f32[128,32]{0,1:T(8,128)}, f32[128,32]{0,1:T(8,128)S(1)}, u32[]{:S(2)}) copy-start(f32[128,32]{0,1:T(8,128)S(1)} %get-tuple-element.479) | copy-start | bytes 49156
  67.4 128.7 %copy-start.26 = (bf16[1,128,1024]{2,1,0:T(8,128)(2,1)S(1)}, bf16[1,128,1024]{2,1,0:T(8,128)(2,1)}, u32[]{:S(2)}) copy-start(bf16[1,128,1024]{2,1,0:T(8,128)(2,1)} %param.21) | copy-start | bytes 786436
  71.2 196.4 %all-gather.12.cloned.1.call-start = ((), (), s32[]{:S(2)}) async-start(), calls=%async_computation.10 | async-start | bytes 2228224 | tf_op jit(solution)/shard_map/all_gather | solution.py:127
  125.3 200.5 %all-gather.20.cloned.1.call-start = ((), (), s32[]{:S(2)}) async-start(), calls=%async_computation.14 | async-start | bytes 2162688 | tf_op jit(solution)/shard_map/all_gather | solution.py:106
  125.9 316.6 %all-gather.24.cloned.1.call-start = ((), (), s32[]{:S(2)}) async-start(), calls=%async_computation.16 | async-start | bytes 17301504 | tf_op jit(solution)/shard_map/all_gather | solution.py:182
  126.6 511.9 %all-gather.22.cloned.1.call-start = ((), (), s32[]{:S(2)}) async-start(), calls=%async_computation.15 | async-start | bytes 34603008 | tf_op jit(solution)/shard_map/all_gather | solution.py:181
  127.4 771.7 %reduce-scatter.14.cloned.1.call-start = ((), (), s32[]{:S(2)}) async-start(), calls=%async_computation.18 | async-start | bytes 4456448 | tf_op jit(solution)/shard_map/reduce_scatter | solution.py:281
  127.7 200.2 %copy-start.40 = (f32[1024]{0:T(1024)}, f32[1024]{0:T(1024)S(1)}, u32[]{:S(2)}) copy-start(f32[1024]{0:T(1024)S(1)} %convert_element_type.132) | copy-start | bytes 12292
  195.9 132.7 %copy-start.33 = (bf16[1024,16]{0,1:T(8,128)(2,1)}, bf16[1024,16]{0,1:T(8,128)(2,1)S(1)}, u32[]{:S(2)}) copy-start(bf16[1024,16]{0,1:T(8,128)(2,1)S(1)} %reshape.456) | copy-start | bytes 98308
  296.7 31.9 copy-start.36
  296.7 31.9 copy-start.38
  297.8 167.2 %copy-start.17 = (bf16[128,8,2,64]{0,3,2,1:T(8,128)(2,1)}, bf16[128,8,2,64]{0,3,2,1:T(8,128)(2,1)S(1)}, u32[]{:S(2)}) copy-start(bf16[128,8,2,64]{0,3,2,1:T(8,128)(2,1)S(1)} %convert_element_type.130) | copy-start | bytes 786436
  327.9 431.8 %copy-start.9 = (f32[128,1024]{1,0:T(8,128)}, f32[128,1024]{1,0:T(8,128)S(1)}, u32[]{:S(2)}) copy-start(f32[128,1024]{1,0:T(8,128)S(1)} %get-tuple-element.483) | copy-start | bytes 1572868
  328.7 353.9 %copy-start.13 = (bf16[128,1024]{1,0:T(8,128)(2,1)}, bf16[128,1024]{1,0:T(8,128)(2,1)S(1)}, u32[]{:S(2)}) copy-start(bf16[128,1024]{1,0:T(8,128)(2,1)S(1)} %multiply_convert_fusion.5) | copy-start | bytes 786436
  706.7 9.1 copy-start.5
  706.7 9.1 copy-start.24
  715.8 14.7 copy-start.3
  745.5 14.2 copy-start.34
  745.5 14.2 copy-start.41
  745.5 14.2 copy-start.48
  761.5 12.8 copy-start.10
  761.5 12.8 copy-start.23
  761.5 12.8 copy-start.27
  761.5 13.8 copy-start.12
  774.3 5.6 copy-start.4
  774.3 5.6 copy-start.37
  774.3 5.6 copy-start.39
  774.3 5.6 copy-start.46
  780.1 12.5 copy-start.1
  781.7 3.4 copy-start.21
  792.6 3.4 copy-start
  799.3 4.8 copy-start.2
  804.1 12.5 copy-start.1
  805.7 3.4 copy-start.21
  816.6 3.4 copy-start
  823.3 4.8 copy-start.2
  828.1 2.1 copy-start.18
  828.1 146.8 %reduce-scatter.12.cloned.1.call-start = ((), (), s32[]{:S(2)}) async-start(), calls=%async_computation.17 | async-start | bytes 4456448 | tf_op jit(solution)/shard_map/reduce_scatter | solution.py:278
  828.7 291.2 %reduce-scatter.28.cloned.1.call-start = ((), (), s32[]{:S(2)}) async-start(), calls=%async_computation.25 | async-start | bytes 540672
  830.1 3.0 copy-start.30
  830.1 3.0 copy-start.35
  830.1 3.1 copy-start.8
  830.1 3.1 copy-start.32
  830.1 3.1 copy-start.43
  830.2 420.6 %reduce-scatter.22.cloned.1.call-start = ((), (), s32[]{:S(2)}) async-start(), calls=%async_computation.22 | async-start | bytes 4325376 | tf_op jit(solution)/shard_map/reduce_scatter | solution.py:323
  833.0 559.0 %reduce-scatter.16.cloned.1.call-start = ((), (), s32[]{:S(2)}) async-start(), calls=%async_computation.19 | async-start | bytes 4325376 | tf_op jit(solution)/shard_map/reduce_scatter | solution.py:320
  833.2 2.9 copy-start.19
  836.1 692.1 %reduce-scatter.20.cloned.1.call-start = ((), (), s32[]{:S(2)}) async-start(), calls=%async_computation.21 | async-start | bytes 2162688 | tf_op jit(solution)/shard_map/reduce_scatter | solution.py:322
  901.9 77.9 %copy-start.6 = (bf16[128,16,512]{2,0,1:T(8,128)(2,1)S(1)}, bf16[128,16,512]{2,0,1:T(8,128)(2,1)}, u32[]{:S(2)}) copy-start(bf16[128,16,512]{2,0,1:T(8,128)(2,1)} %copy-done.5) | copy-start | bytes 6291460
  901.9 77.9 %copy-start.16 = (f32[128,1024]{1,0:T(8,128)S(1)}, f32[128,1024]{1,0:T(8,128)}, u32[]{:S(2)}) copy-start(f32[128,1024]{1,0:T(8,128)} %get-tuple-element.475) | copy-start | bytes 1572868
  901.9 762.3 %reduce-scatter.18.cloned.1.call-start = ((), (), s32[]{:S(2)}) async-start(), calls=%async_computation.20 | async-start | bytes 2162688 | tf_op jit(solution)/shard_map/reduce_scatter | solution.py:321
  979.7 1389.6 %reduce-scatter.26.cloned.1.call-start = ((), (), s32[]{:S(2)}) async-start(), calls=%async_computation.24 | async-start | bytes 34603008 | tf_op jit(solution)/shard_map/reduce_scatter | solution.py:221
  1024.4 2751.7 %reduce-scatter.24.cloned.1.call-start = ((), (), s32[]{:S(2)}) async-start(), calls=%async_computation.23 | async-start | bytes 69206016 | tf_op jit(solution)/shard_map/reduce_scatter | solution.py:218
  1116.8 8.3 copy-start.44
  (10 other events, 11.4 us)
Sparse Core Ops, SparseCore 0:
  10.9 56.4 all-gather.13
  70.3 52.6 all-gather.9
  126.1 55.7 all-gather.17
  184.5 40.0 all-gather.15
  227.2 40.3 all-gather.11
  270.5 55.2 all-gather.19
  328.7 113.7 all-gather.23
  445.5 192.9 all-gather.21
  828.3 70.7 reduce-scatter.13
  903.2 71.6 reduce-scatter.11
  977.2 133.1 reduce-scatter.27
  1113.2 137.5 reduce-scatter.21
  1253.7 138.2 reduce-scatter.15
  1394.8 133.3 reduce-scatter.19
  1530.9 133.2 reduce-scatter.17
  1667.0 702.3 reduce-scatter.25
  2372.2 1403.8 reduce-scatter.23
where the time goes:
time: 3790 us; the launch traced here: 3780 us
  waiting for transfers between devices  3190 us (84%)
  local copies, waits for them, and re-layouts  221 us (6%)
  matrix products  188 us (5%)
  blocking collectives  150 us (4%)
    reduce_scatter x1, waiting for transfers between devices, per_device(): lax.psum_scatter(grad_gate_up.reshape(D, E * 2 * F), ('ctx', 'fsdp'), sca...  1410 us
    reduce_scatter x1, waiting for transfers between devices, per_device(): lax.psum_scatter(grad_down.reshape(D, E * F), ('ctx', 'fsdp'), scatter_di...  705 us
    all_gather x1, waiting for transfers between devices, per_device(): lax.all_gather(w_gate_up, ('ctx', 'fsdp'), axis=0, tiled=True)  174 us
    reduce_scatter x1, waiting for transfers between devices, per_device(): lax.psum_scatter(grad_query, ('ctx', 'fsdp'), scatter_dimension=0, tiled=...  141 us
    reduce_scatter x1, waiting for transfers between devices, per_device(): lax.psum_scatter(grad_value, ('ctx', 'fsdp'), scatter_dimension=0, tiled=...  136 us
    reduce_scatter x1, waiting for transfers between devices, per_device(): lax.psum_scatter(grad_key, ('ctx', 'fsdp'), scatter_dimension=0, tiled=True)  136 us
    all_gather x1, waiting for transfers between devices, per_device(): lax.all_gather(w_down, ('ctx', 'fsdp'), axis=0, tiled=True)  113 us
    reduce_scatter x1, waiting for transfers between devices, per_device(): lax.psum_scatter(grad_output, ('ctx', 'fsdp'), scatter_dimension=0, tiled...  83 us
  transfers between devices with their start and end apart: 17, of which 15 were waited for; matrix products, arithmetic and copies ran while one was open for 6% of the time, Pallas kernels for 0%

commit v1 on v0

v1 whole, which is shorter than its diff:
```python
import functools

import jax
import jax.numpy as jnp
import numpy as np
from jax import lax
from jax.experimental import pallas as pl
from jax.experimental.pallas import tpu as pltpu
from jax.sharding import PartitionSpec as P

D = 1024
H = 16
KVH = 8
HD = 64
F = 512
E = 16

EPSILON = 1e-06
SCORE_SCALE = 0.015625
RESIDUAL_SCALE = 0.22
THETA = 10000.0
NEGATIVE = -1e30
BOTH = ("ctx", "fsdp")
BF = jnp.bfloat16
F32 = jnp.float32
QUERY_BLOCK = 256


def dot(left, right, left_dim, right_dim):
    return lax.dot_general(
        left, right, (((left_dim,), (right_dim,)), ((), ())), preferred_element_type=F32
    )


def permute(values, pairs):
    return lax.ppermute(values, "ctx", pairs)


def shift_z(step):
    return [(i, ((i // 4 + step) % 4) * 4 + i % 4) for i in range(16)]


SWAP_X = [(i, i ^ 2) for i in range(16)]
SWAP_CORE = [(i, i ^ 1) for i in range(16)]


def after(value, *others):
    return lax.optimization_barrier((value, *others))[0] if others else lax.optimization_barrier(value)


def block_order_of(count):
    index = jnp.arange(count, dtype=jnp.int32)
    if lax.axis_size("ctx") != 16:
        return index
    place = lax.axis_index("ctx")
    z_of = (place // 4 - (index % 8) // 2 + 4) % 4
    x_of = ((place // 2) % 2 + index % 2) % 2
    return z_of * 4 + x_of * 2 + (place % 2 + index // 8) % 2


class RingSum:
    def __init__(self, mine, arrived):
        self.mine, self.arrived = mine, arrived
        self.count = mine.shape[0] // 8
        self.cross_out = jnp.concatenate([self.chip(k, 1) for k in (2, 1, 3)], 0).astype(BF)

    def chip(self, k, dx):
        rows = slice((2 * k + dx) * self.count, (2 * k + dx + 1) * self.count)
        return self.mine[rows].astype(F32) + self.arrived[rows].astype(F32)

    def cross(self):
        got = permute(self.cross_out, SWAP_X)
        self.sends = []
        for j, k in enumerate((2, 1, 3)):
            term = got[j * self.count : (j + 1) * self.count].astype(F32)
            self.sends.append((self.chip(k, 0) + term).astype(BF))

    def end(self, *others):
        self.own = permute(self.chip(0, 1).astype(BF), SWAP_X)
        total = self.chip(0, 0) + self.own.astype(F32)
        for send, k in zip(self.sends, (2, 1, 3)):
            term = permute(send, shift_z(4 - k))
            if k == 2 and others:
                term = after(term, *others)
            total = total + term.astype(F32)
        return total


def join_kernel(places, *refs):
    pieces, out_ref, sems = refs[:14], refs[14], refs[15]
    count = out_ref.shape[1]
    copies = []
    for side in range(2):
        own, far, one, pair, two, far_two, three = pieces[7 * side : 7 * side + 7]
        lower, upper = pair.at[:count], pair.at[count:]
        for j, piece in enumerate((own, far, one, lower, two, far_two, three, upper)):
            block = 8 * side + j
            copies.append(
                pltpu.make_async_copy(piece, out_ref.at[places[block]], sems.at[block])
            )
    for copy in copies:
        copy.start()
    for copy in copies:
        copy.wait()


class Gather:
    def __init__(self, rows):
        self.count = rows.shape[0]
        self.own = rows
        self.one = permute(rows, shift_z(1))
        self.three = permute(rows, shift_z(3))
        self.far = permute(rows, SWAP_X)
        self.two = permute(rows, shift_z(2))

    def cross(self, *others):
        if others:
            self.one, self.three = after((self.one, self.three), *others)
        self.pair = permute(jnp.concatenate([self.one, self.three], 0), SWAP_X)

    def last(self, *others):
        if others:
            self.two = after(self.two, *others)
        self.far_two = permute(self.two, SWAP_X)

    def join(self, places, name, *others):
        if others:
            self.far, self.far_two = after((self.far, self.far_two), *others)
        mine = (self.own, self.far, self.one, self.pair, self.two, self.far_two, self.three)
        other = tuple(permute(piece, SWAP_CORE) for piece in mine)
        shape = (16, *self.own.shape)
        return pl.pallas_call(
            join_kernel,
            out_shape=jax.ShapeDtypeStruct(shape, BF),
            grid_spec=pltpu.PrefetchScalarGridSpec(
                num_scalar_prefetch=1,
                grid=(1,),
                in_specs=[fixed(piece.shape) for piece in (*mine, *other)],
                out_specs=pl.BlockSpec(memory_space=pl.ANY),
                scratch_shapes=[pltpu.SemaphoreType.DMA((16,))],
            ),
            compiler_params=params(),
            cost_estimate=cost(1, 4 * self.own.size * 16),
            name=name,
        )(places, *mine, *other)


def tables_of(total):
    half_width = HD // 2
    frequency = (THETA ** (-np.arange(half_width) / half_width)).astype(np.float32)
    angles = np.arange(total, dtype=np.float32)[:, None] * frequency[None, :]
    cosine = np.cos(angles.astype(np.float64)).astype(np.float32)
    sine = np.sin(angles.astype(np.float64)).astype(np.float32)
    return jnp.asarray(np.tile(cosine, (1, 4))), jnp.asarray(np.tile(sine, (1, 4)))


def window_of(step, band):
    start = jnp.maximum(step * QUERY_BLOCK - band, 0)
    return pl.multiple_of(start, QUERY_BLOCK), pl.multiple_of(step * QUERY_BLOCK, QUERY_BLOCK)


def masked_scores(queries, keys_win, first_key, first_query, firsts):
    raw = dot(queries, keys_win, 1, 1) * SCORE_SCALE
    key_place = first_key + lax.broadcasted_iota(jnp.int32, raw.shape, 1)
    query_place = first_query + lax.broadcasted_iota(jnp.int32, raw.shape, 0)
    column = first_query + lax.broadcasted_iota(jnp.int32, (raw.shape[0], 1), 0)
    start = jnp.zeros_like(column)
    for j in range(1, firsts.shape[0]):
        start = jnp.where(firsts[j] <= column, jnp.maximum(start, firsts[j]), start)
    visible = (key_place <= query_place) & (key_place >= start)
    return jnp.where(visible, raw, NEGATIVE)


def lanes_of(values):
    return lax.broadcasted_iota(jnp.int32, values.shape, 1)


def fixed(shape, at=None):
    place = (0,) * len(shape) if at is None else at
    return pl.BlockSpec(shape, lambda *_: place, pipeline_mode=pl.Buffered(1))


def params(mib=56):
    return pltpu.CompilerParams(vmem_limit_bytes=mib * 2**20)


def cost(flops, bytes_accessed, transcendentals=0, weight=20):
    return pl.CostEstimate(
        flops=weight * flops,
        bytes_accessed=weight * bytes_accessed,
        transcendentals=transcendentals,
    )


def column_of(row_ref):
    return jnp.broadcast_to(row_ref[:1, :], (128, row_ref.shape[1])).T


def pack_kernel(copies, wq_ref, wk_ref, wv_ref, wr_ref, norm_ref, small_ref):
    rows = wq_ref.shape[0]
    rest = jnp.concatenate(
        [wr_ref[...], norm_ref[...], jnp.zeros((rows, HD - E - 2), BF)], axis=1
    )
    for place in range(E * copies):
        head = place // copies
        pair = head // (H // KVH)
        query = wq_ref[:, head * HD : (head + 1) * HD]
        key = wk_ref[:, pair * HD : (pair + 1) * HD]
        value = wv_ref[:, pair * HD : (pair + 1) * HD]
        small_ref[place] = jnp.concatenate([query, key, value, rest], axis=1)


def pack_small(copies, *weights):
    shape = (E * copies, weights[0].shape[0], 256)
    return pl.pallas_call(
        functools.partial(pack_kernel, copies),
        out_shape=jax.ShapeDtypeStruct(shape, BF),
        grid=(1,),
        in_specs=[fixed(weight.shape) for weight in weights],
        out_specs=fixed(shape),
        compiler_params=params(),
        cost_estimate=cost(1, 2**20),
        name="pack_small",
    )(*weights)


def split_kernel(small_ref, ext_ref, head_ref, router_ref, one_ref, two_ref):
    small = small_ref[...]
    wq, wk, wv = (small[:, j * HD : (j + 1) * HD] for j in range(3))
    turn = HD // 2
    zero = jnp.zeros_like(wv)
    rest = small[:, 3 * HD :]
    ext_ref[:, :128] = small[:, :128]
    ext_ref[:, 128:256] = jnp.concatenate(
        [-wq[:, turn:], wq[:, :turn], -wk[:, turn:], wk[:, :turn]], 1
    )
    value = jnp.concatenate([wv, zero], 1)
    ext_ref[:, 256:] = value
    head_ref[:, :128] = small[:, :128]
    head_ref[:, 128:] = value
    rest = jnp.concatenate([rest, zero], 1).astype(F32)
    router_ref[...] = jnp.where(lanes_of(rest) < E, rest, 0.0).astype(BF)
    turned = rest.T
    one_ref[...] = turned[E : E + 1, :]
    two_ref[...] = turned[E + 1 : E + 2, :]


def split_small(small):
    shapes = ((D, 384), (D, 256), (D, 128), (1, D), (1, D))
    types = (BF, BF, BF, F32, F32)
    return pl.pallas_call(
        split_kernel,
        out_shape=tuple(jax.ShapeDtypeStruct(s, t) for s, t in zip(shapes, types)),
        grid=(1,),
        in_specs=[fixed(small.shape)],
        out_specs=tuple(fixed(s) for s in shapes),
        compiler_params=params(),
        cost_estimate=cost(1, 3 * 2**20),
        name="split_weights",
    )(small)


def project(x_blk, w_ref, gain_ref, cosine, sine):
    x_f = x_blk.astype(F32)
    factor = lax.rsqrt(jnp.mean(x_f * x_f, axis=1, keepdims=True) + EPSILON)
    normed = (x_f * factor * gain_ref[...]).astype(BF)
    out = dot(normed, w_ref[...], 1, 0)
    both = out[:, :128] * cosine + out[:, 128:256] * sine
    swapped = pltpu.roll(both, 64, 1)
    low = lanes_of(both) < HD
    zero = jnp.zeros_like(both)
    return jnp.concatenate(
        [
            jnp.where(low, both, zero).astype(BF),
            jnp.where(low, swapped, zero).astype(BF),
            jnp.where(low, zero, swapped).astype(BF),
            out[:, 256:].astype(BF),
        ],
        axis=1,
    )


def spot_of(ids, block, block_len):
    return pl.ds(pl.multiple_of(ids[block] * block_len, block_len), block_len)


def head_kernel(
    block_len, band, ids, spots, firsts,
    x_ref, w_ref, gain_ref, cos_ref, sin_ref, all_ref, log_ref, att_ref, a_store,
):
    step = pl.program_id(0)
    total = all_ref.shape[0]
    blocks = QUERY_BLOCK // block_len

    places = [spot_of(ids, 4 * step + j, block_len) for j in range(4)]
    cosine = jnp.concatenate([cos_ref[spot, :] for spot in places], 0)
    sine = jnp.concatenate([sin_ref[spot, :] for spot in places], 0)
    made = project(x_ref[...], w_ref, gain_ref, cosine, sine)
    for j in range(4):
        all_ref[places[j], :] = made[j * block_len : (j + 1) * block_len]

    @pl.when(step == pl.num_programs(0) - 1)
    def _():
        window = band + QUERY_BLOCK

        def step_fn(index, carry):
            first_key, first_query = window_of(index, band)
            rows = pl.ds(first_query, QUERY_BLOCK)
            cols = pl.ds(first_key, window)
            scores = masked_scores(
                all_ref[rows, :128], all_ref[cols, 128:256], first_key, first_query, firsts
            )
            top = jnp.max(scores, axis=1, keepdims=True)
            weight = jnp.exp(scores - top)
            mass = jnp.sum(weight, axis=1, keepdims=True)
            log_ref[rows, :] = top + jnp.log(mass)
            weight = (weight * (1.0 / mass)).astype(BF)
            result = dot(weight, all_ref[cols, 384:], 1, 0)
            for j in range(blocks):
                spot = spot_of(spots, index * blocks + j, block_len)
                a_store[spot, :] = result[j * block_len : (j + 1) * block_len]
            return carry

        lax.fori_loop(0, total // QUERY_BLOCK, step_fn, 0)
        for j in range(total // QUERY_BLOCK):
            part = a_store[j * QUERY_BLOCK : (j + 1) * QUERY_BLOCK, :]
            att_ref[:, j * QUERY_BLOCK : (j + 1) * QUERY_BLOCK] = part.T[:HD].astype(BF)


def head_forward(hidden, w_ext, gain, tables, ids, spots, firsts, count, band):
    total = tables[0].shape[0]
    work = total * (band + QUERY_BLOCK)
    return pl.pallas_call(
        functools.partial(head_kernel, count // 2, band),
        out_shape=(
            jax.ShapeDtypeStruct((total, 512), BF),
            jax.ShapeDtypeStruct((total, 1), F32),
            jax.ShapeDtypeStruct((HD, total), BF),
        ),
        grid_spec=pltpu.PrefetchScalarGridSpec(
            num_scalar_prefetch=3,
            grid=(total // count // 2,),
            in_specs=[
                pl.BlockSpec((2 * count, D), lambda i, *_: (i, 0)),
                fixed((D, 384)), fixed((1, D)), fixed((total, 128)), fixed((total, 128)),
            ],
            out_specs=(fixed((total, 512)), fixed((total, 1)), fixed((HD, total))),
            scratch_shapes=[pltpu.VMEM((total, 128), F32)],
        ),
        compiler_params=params(),
        cost_estimate=cost(total * D * 384 + 4 * work * 128, 2 * total * D, work),
        name="head_forward",
    )(ids, spots, firsts, hidden, w_ext, gain, *tables)


def order_heads(heads, wo_ref, wo_rel):
    per = wo_ref.shape[1]
    many = HD // per
    for j in range(H):
        for m in range(many):
            wo_rel[j * HD + m * per : j * HD + (m + 1) * per, :] = wo_ref[heads[j] * many + m]


def front_kernel(
    tok_count, where, att_ref, x_ref, wo_ref, wgu_ref, gain_ref, mixed_ref, gates_ref, factor_ref,
    mid_ref, scr,
):
    step = pl.program_id(0)
    tile = x_ref.shape[0]
    moved = dot(att_ref[...].reshape(D, tile), wo_ref[...].reshape(D, D), 0, 0)
    middle = x_ref[...].astype(F32) + RESIDUAL_SCALE * moved
    scr[...] = middle

    @pl.when(step == where[2] * tok_count // tile)
    def _():
        own = pl.multiple_of(where[2] * tok_count % tile, tok_count)
        mid_ref[...] = scr[pl.ds(own, tok_count), :]

    factor = lax.rsqrt(jnp.mean(middle * middle, axis=1, keepdims=True) + EPSILON)
    factor_ref[...] = jnp.broadcast_to(factor, factor_ref.shape)
    mixed = (middle * factor * gain_ref[...]).astype(BF)
    mixed_ref[...] = mixed
    gates_ref[...] = dot(mixed, wgu_ref[...], 1, 0)


def expert_front(att, hidden, wo, wgu, gain, where, count):
    total = hidden.shape[0]
    wide = wgu.shape[1]
    tile = 4 * count

    def rows(width):
        return pl.BlockSpec((tile, width), lambda i, *_: (i, 0))

    return pl.pallas_call(
        functools.partial(front_kernel, count),
        out_shape=(
            jax.ShapeDtypeStruct((total, D), BF),
            jax.ShapeDtypeStruct((total, wide), F32),
            jax.ShapeDtypeStruct((total, 128), F32),
            jax.ShapeDtypeStruct((count, D), F32),
        ),
        grid_spec=pltpu.PrefetchScalarGridSpec(
            num_scalar_prefetch=1,
            grid=(total // tile,),
            in_specs=[
                pl.BlockSpec((H, HD, tile), lambda i, *_: (0, 0, i)),
                rows(D), fixed(wo.shape), fixed((D, wide)), fixed((1, D)),
            ],
            out_specs=(rows(D), rows(wide), rows(128), fixed((count, D))),
            scratch_shapes=[pltpu.VMEM((tile, D), F32)],
        ),
        compiler_params=params(),
        cost_estimate=cost(2 * total * D * (D + wide), 14 * total * D),
        name="expert_front",
    )(where, att, hidden, wo, wgu, gain)


def back_kernel(
    part, heads, where, mixed_ref, gates_ref, factor_ref, g_ref, wo_ref, wgu_ref, wd_ref, wr_ref,
    gain_ref, gb_ref, act_ref, v_ref, coef_ref, pa_ref, pb_ref, norm_ref, wo_rel,
):
    step = pl.program_id(0)
    own_expert = where[0]
    half = D // 2

    @pl.when(step == 0)
    def _():
        order_heads(heads, wo_ref, wo_rel)
        norm_ref[...] = jnp.zeros_like(norm_ref)

    mixed = mixed_ref[...]
    grads = g_ref[...].reshape(mixed.shape[0], D + 128)
    logits = dot(mixed, wr_ref[...], 1, 0)
    mask = grads[:, D:].astype(F32)
    logits = jnp.where(mask > 0.0, logits, NEGATIVE)
    odds = jnp.where(mask > 0.0, jnp.exp(logits - jnp.max(logits, axis=1, keepdims=True)), 0.0)
    combine = odds / jnp.sum(odds, axis=1, keepdims=True)
    mark = (lanes_of(combine) == own_expert).astype(F32)
    own_gate = jnp.sum(combine * mark, axis=1, keepdims=True)
    grad_top = grads[:, :D]
    pulled = RESIDUAL_SCALE * dot(grad_top, wd_ref[...], 1, 0)
    gate, up = gates_ref[:, :part], gates_ref[:, part:]
    sigma = 1.0 / (1.0 + jnp.exp(-gate))
    silu = gate * sigma
    activation = silu * up
    grad_act = own_gate * pulled
    act_ref[...] = (RESIDUAL_SCALE * own_gate * activation).astype(BF)
    gb_ref[:, :part] = (grad_act * up * sigma * (1.0 + gate * (1.0 - sigma))).astype(BF)
    gb_ref[:, part:] = (grad_act * silu).astype(BF)
    grad_combine = jnp.sum(activation * pulled, axis=1, keepdims=True)
    coef = (grad_combine * own_gate * (mark - combine)).astype(BF)
    coef_ref[...] = coef
    grad_mixed = dot(gb_ref[...], wgu_ref[...], 1, 1) + dot(coef, wr_ref[...], 1, 1)
    gain = gain_ref[...]
    scaled = mixed.astype(F32) * (1.0 / gain)
    norm_ref[...] += jnp.broadcast_to(
        jnp.sum(grad_mixed * scaled, axis=0, keepdims=True), norm_ref.shape
    )
    inner = grad_mixed * gain
    factor = factor_ref[:, :1]
    grad_mid = factor * (inner - scaled * jnp.mean(inner * scaled, axis=1, keepdims=True))
    grad_mid = grad_mid.astype(BF)
    v_ref[...] = grad_mid
    out_grads = dot(wo_rel[...], grad_mid, 1, 1)
    if part == F:
        top = out_grads[:HD] + dot(wo_rel[:HD, :], grad_top, 1, 1)
        pa_ref[:HD, :] = (RESIDUAL_SCALE * top).astype(BF)
        pa_ref[HD:, :] = (RESIDUAL_SCALE * out_grads[HD:half]).astype(BF)
    else:
        pa_ref[...] = (RESIDUAL_SCALE * out_grads[:half]).astype(BF)
    pb_ref[...] = (RESIDUAL_SCALE * out_grads[half:]).astype(BF)


def expert_back(
    mixed, gates, factor, top, wo, wgu, wd, wr, gain, heads, where, count
):
    total = mixed.shape[0]
    part = wd.shape[1]
    tile = 2 * count

    def rows(width):
        return pl.BlockSpec((tile, width), lambda i, *_: (i, 0))

    def cols(height):
        return pl.BlockSpec((height, tile), lambda i, *_: (0, i))

    def out(width):
        return jax.ShapeDtypeStruct((total, width), BF)

    half = jax.ShapeDtypeStruct((D // 2, total), BF)
    return pl.pallas_call(
        functools.partial(back_kernel, part),
        out_shape=(
            out(2 * part), out(part), out(D), out(128), half, half,
            jax.ShapeDtypeStruct((8, D), F32),
        ),
        grid_spec=pltpu.PrefetchScalarGridSpec(
            num_scalar_prefetch=2,
            grid=(total // tile,),
            in_specs=[
                rows(D), rows(2 * part), rows(128),
                pl.BlockSpec((2, count, D + 128), lambda i, *_: (i, 0, 0)),
                fixed(wo.shape), fixed((D, 2 * part)), fixed((D, part)), fixed((D, 128)),
                fixed((1, D)),
            ],
            out_specs=(
                rows(2 * part), rows(part), rows(D), rows(128), cols(D // 2), cols(D // 2),
                fixed((8, D)),
            ),
            scratch_shapes=[pltpu.VMEM((D, D), BF)],
        ),
        compiler_params=params(),
        cost_estimate=cost(2 * total * D * (D + 3 * part), 14 * total * D, total * part),
        name="expert_back",
    )(heads, where, mixed, gates, factor, top, wo, wgu, wd, wr, gain)


def up_kernel(mixed_ref, gb_ref, coef_ref, norm_ref, out_ref, acc):
    step = pl.program_id(0)
    wide = gb_ref.shape[1]
    terms = ((0, wide, gb_ref[...]), (wide, wide + 128, coef_ref[...]))

    @pl.when(step == 0)
    def _():
        for low, high, right in terms:
            acc[:, low:high] = dot(mixed_ref[...], right, 0, 0)

    @pl.when(step > 0)
    def _():
        for low, high, right in terms:
            acc[:, low:high] += dot(mixed_ref[...], right, 0, 0)

    @pl.when(step == pl.num_programs(0) - 1)
    def _():
        out_ref[:, :wide] = acc[:, :wide].astype(BF)
        last = acc[:, wide:]
        out_ref[:, wide:] = jnp.where(lanes_of(last) == E, column_of(norm_ref), last).astype(BF)


def up_weights(mixed, gb, coef, norm):
    total, wide = gb.shape
    tile = 512

    def rows(size):
        return pl.BlockSpec((tile, size), lambda i: (i, 0))

    return pl.pallas_call(
        up_kernel,
        out_shape=jax.ShapeDtypeStruct((D, wide + 128), BF),
        grid=(total // tile,),
        in_specs=[rows(D), rows(wide), rows(128), fixed((8, D))],
        out_specs=fixed((D, wide + 128)),
        scratch_shapes=[pltpu.VMEM((D, wide + 128), F32)],
        compiler_params=params(),
        cost_estimate=cost(2 * total * D * wide, 4 * total * D),
        name="up_weights",
    )(mixed, gb, coef, norm)


def down_kernel(g_ref, act_ref, out_ref, acc):
    step = pl.program_id(0)
    grads = g_ref[...].reshape(-1, D)

    @pl.when(step == 0)
    def _():
        acc[...] = dot(grads, act_ref[...], 0, 0)

    @pl.when(step > 0)
    def _():
        acc[...] += dot(grads, act_ref[...], 0, 0)

    @pl.when(step == pl.num_programs(0) - 1)
    def _():
        out_ref[...] = acc[...].astype(BF)


def down_weights(both, act, count):
    total, part = act.shape
    return pl.pallas_call(
        down_kernel,
        out_shape=jax.ShapeDtypeStruct((D, part), BF),
        grid=(total // (4 * count),),
        in_specs=[
            pl.BlockSpec((4, count, D), lambda i: (i, 0, 0)),
            pl.BlockSpec((4 * count, part), lambda i: (i, 0)),
        ],
        out_specs=fixed((D, part)),
        scratch_shapes=[pltpu.VMEM((D, part), F32)],
        compiler_params=params(),
        cost_estimate=cost(2 * total * D * part, 3 * total * D),
        name="down_weights",
    )(both, act)


def moe_kernel(act_ref, wd_ref, out_ref):
    out_ref[...] = dot(act_ref[...], wd_ref[...], 1, 1).astype(BF).reshape(out_ref.shape)


def moe_out(act, wd, count, rows):
    total, part = act.shape
    many = 4
    return pl.pallas_call(
        moe_kernel,
        out_shape=jax.ShapeDtypeStruct((total // count, count + 2 * rows, D), BF),
        grid=(total // count // many,),
        in_specs=[pl.BlockSpec((many * count, part), lambda i: (i, 0)), fixed((D, part))],
        out_specs=pl.BlockSpec((many, count, D), lambda i: (i, 0, 0)),
        compiler_params=params(),
        cost_estimate=cost(2 * total * D * part, 3 * total * D),
        name="moe_out",
    )(act, wd)


def output_kernel(where, att_ref, v_ref, g_ref, moe_ref, out_ref, acc):
    step = pl.program_id(0)
    tile = v_ref.shape[0]

    @pl.when(step == 0)
    def _():
        acc[...] = jnp.zeros_like(acc)

    acc[...] += dot(att_ref[...].reshape(D, tile), v_ref[...], 1, 0)
    picked = att_ref[where[0]]
    place = step * tile + lanes_of(picked)
    picked = jnp.where(place // where[3] == where[1], picked, jnp.zeros_like(picked))
    target = pl.ds(pl.multiple_of(where[0] * HD, HD), HD)
    acc[target, :] += dot(picked, g_ref[...].reshape(tile, D), 1, 0)

    @pl.when(step == pl.num_programs(0) - 1)
    def _():
        out_ref[...] = (RESIDUAL_SCALE * acc[...]).astype(BF).reshape(out_ref.shape)


def output_weights(att, grad_mid, top, moe, where, count, rows):
    total = grad_mid.shape[0]
    tile = 4 * count
    per = 2 * rows
    return pl.pallas_call(
        output_kernel,
        out_shape=jax.ShapeDtypeStruct(moe.shape, BF),
        grid_spec=pltpu.PrefetchScalarGridSpec(
            num_scalar_prefetch=1,
            grid=(total // tile,),
            in_specs=[
                pl.BlockSpec((H, HD, tile), lambda i, *_: (0, 0, i)),
                pl.BlockSpec((tile, D), lambda i, *_: (i, 0)),
                pl.BlockSpec((4, count, D), lambda i, *_: (i, 0, 0)),
                pl.BlockSpec(memory_space=pl.ANY),
            ],
            out_specs=fixed((moe.shape[0], per, D), (0, count // per, 0)),
            scratch_shapes=[pltpu.VMEM((D, D), F32)],
        ),
        input_output_aliases={4: 0},
        compiler_params=params(),
        cost_estimate=cost(2 * total * D * D, 8 * total * D),
        name="output_weights",
    )(where, att, grad_mid, top, moe)


def attend_kernel(
    block_len, band, ids, spots, firsts, where, all_ref, up_ref, log_ref, cos_ref, sin_ref,
    own_ref, up_sort, acc_qk, acc_v,
):
    total = all_ref.shape[0]
    blocks = QUERY_BLOCK // block_len
    window = band + QUERY_BLOCK
    acc_qk[...] = jnp.zeros_like(acc_qk)
    acc_v[...] = jnp.zeros_like(acc_v)
    for j in range(total // QUERY_BLOCK):
        piece = up_ref[:, j * QUERY_BLOCK : (j + 1) * QUERY_BLOCK]
        piece = jnp.concatenate([piece, jnp.zeros_like(piece)], 0).T.astype(BF)
        for m in range(blocks):
            spot = spot_of(ids, j * blocks + m, block_len)
            up_sort[spot, :] = piece[m * block_len : (m + 1) * block_len]

    def step_fn(index, carry):
        first_key, first_query = window_of(index, band)
        rows = pl.ds(first_query, QUERY_BLOCK)
        cols = pl.ds(first_key, window)
        keys_win, upstream = all_ref[cols, 128:256], up_sort[rows, :]
        scores = masked_scores(all_ref[rows, :128], keys_win, first_key, first_query, firsts)
        weight = jnp.exp(scores - log_ref[rows, :])
        grad_weight = dot(upstream, all_ref[cols, 384:], 1, 1)
        delta = jnp.sum(weight * grad_weight, axis=1, keepdims=True)
        grad_raw = (SCORE_SCALE * weight * (grad_weight - delta)).astype(BF)
        acc_qk[rows, :] += dot(grad_raw, keys_win, 1, 0)
        acc_qk[cols, :] += dot(grad_raw, all_ref[rows, 256:384], 0, 0)
        acc_v[cols, :] += dot(weight.astype(BF), upstream, 0, 0)
        return carry

    lax.fori_loop(0, total // QUERY_BLOCK, step_fn, 0)

    def turn(index, carry):
        first = pl.multiple_of(index * QUERY_BLOCK, QUERY_BLOCK)
        rows = pl.ds(first, QUERY_BLOCK)
        both = acc_qk[rows, :]
        low = lanes_of(both) % HD < HD // 2
        swapped = jnp.where(low, pltpu.roll(both, 96, 1), -pltpu.roll(both, 32, 1))
        turned = (both * cos_ref[rows, :] + swapped * sin_ref[rows, :]).astype(BF)
        made = jnp.concatenate([turned, acc_v[rows, :].astype(BF)], 1)
        for j in range(blocks):
            block = spots[index * blocks + j]
            first = pl.multiple_of(block * block_len, block_len)
            piece = made[j * block_len : (j + 1) * block_len]
            keep = first // where[3] == where[1]
            own_ref[pl.ds(first, block_len), :] = jnp.where(keep, piece, jnp.zeros_like(piece))
        return carry

    lax.fori_loop(0, total // QUERY_BLOCK, turn, 0)


def attend_backward(heads_all, upstream, logs, tables, ids, spots, firsts, where, count, band):
    total = heads_all.shape[0]
    work = total * (band + QUERY_BLOCK)
    return pl.pallas_call(
        functools.partial(attend_kernel, count // 2, band),
        out_shape=jax.ShapeDtypeStruct((total, 256), BF),
        grid_spec=pltpu.PrefetchScalarGridSpec(
            num_scalar_prefetch=4,
            grid=(1,),
            in_specs=[
                fixed((total, 512)), fixed((HD, total)), fixed((total, 1)), fixed((total, 128)),
                fixed((total, 128)),
            ],
            out_specs=fixed((total, 256)),
            scratch_shapes=[
                pltpu.VMEM((total, 128), BF),
                pltpu.VMEM((total, 128), F32),
                pltpu.VMEM((total, 128), F32),
            ],
        ),
        compiler_params=params(60),
        cost_estimate=cost(10 * work * 128, 2 * total * 1024, work),
        name="attend_backward",
    )(ids, spots, firsts, where, heads_all, upstream, logs, *tables)


def pull_kernel(
    last, order, g_ref, h_ref, w_ref, gain_ref, x_ref, y_ref, gm_ref, hm_ref, w_in_ref, n_in_ref,
    out_ref, w_out_ref, n_out_ref, acc_w,
):
    step = pl.program_id(0)

    @pl.when(step == 0)
    def _():
        acc_w[...] = w_in_ref[...]
        n_out_ref[...] = n_in_ref[...]

    grads = jnp.concatenate([g_ref[...], h_ref[...]], 0)
    grad_mid = jnp.concatenate([gm_ref[...], hm_ref[...]], 0).astype(F32)
    grad_normed = dot(grads, w_ref[...], 1, 1)
    x_f = jnp.concatenate([x_ref[...], y_ref[...]], 0).astype(F32)
    factor = lax.rsqrt(jnp.mean(x_f * x_f, axis=1, keepdims=True) + EPSILON)
    scaled = x_f * factor
    normed = (scaled * gain_ref[...]).astype(BF)
    acc_w[...] += dot(normed, grads, 0, 0)
    n_out_ref[...] += jnp.broadcast_to(
        jnp.sum(grad_normed * scaled, axis=0, keepdims=True), n_out_ref.shape
    )
    inner = grad_normed * gain_ref[...]
    grad_x = factor * (inner - scaled * jnp.mean(inner * scaled, axis=1, keepdims=True))
    out_ref[...] = (grad_x + grad_mid).astype(BF)

    @pl.when(step == pl.num_programs(0) - 1)
    def _():
        if last:
            tail = acc_w[:, 128:]
            w_out_ref[:, :128] = acc_w[:, :128].astype(BF)
            w_out_ref[:, 128:] = jnp.where(
                lanes_of(tail) == HD, column_of(n_out_ref), tail
            ).astype(BF)
        else:
            w_out_ref[...] = acc_w[...]


def pull_heads(own_grads, w_head, gain, hidden, grad_mid, w_in, n_in, order, count, last):
    total = hidden.shape[0] // 2

    def at(width, j):
        return pl.BlockSpec((count, width), lambda i, order: (order[2 * i + j], 0))

    block = pl.BlockSpec((2 * count, D), lambda i, order: (i, 0))
    return pl.pallas_call(
        functools.partial(pull_kernel, last),
        out_shape=(
            jax.ShapeDtypeStruct((total, D), BF),
            jax.ShapeDtypeStruct((D, 256), BF if last else F32),
            jax.ShapeDtypeStruct((8, D), F32),
        ),
        grid_spec=pltpu.PrefetchScalarGridSpec(
            num_scalar_prefetch=1,
            grid=(total // count // 2,),
            in_specs=[
                at(256, 0), at(256, 1), fixed((D, 256)), fixed((1, D)), at(D, 0), at(D, 1), at(D, 0),
                at(D, 1),
                fixed((D, 256)), fixed((8, D)),
            ],
            out_specs=(block, fixed((D, 256)), fixed((8, D))),
            scratch_shapes=[pltpu.VMEM((D, 256), F32)],
        ),
        compiler_params=params(),
        cost_estimate=cost(4 * total * D * 256, 6 * total * D, weight=1),
        name="pull_last" if last else "pull_first",
    )(
        order, own_grads, own_grads, w_head, gain, hidden, hidden, grad_mid, grad_mid, w_in, n_in
    )


def finish_kernel(in_ref, q_ref, k_ref, v_ref, gain_ref):
    def piece(head):
        return in_ref[2 * head].astype(F32) + in_ref[2 * head + 1].astype(F32)

    total = jnp.zeros_like(piece(0))
    for quad in range(H // 4):
        heads = [piece(4 * quad + j) for j in range(4)]
        for j in range(2):
            first = (4 * quad + 2 * j) * HD
            q_ref[:, first : first + 128] = jnp.concatenate(
                [heads[2 * j][:, :HD], heads[2 * j + 1][:, :HD]], 1
            )
        pairs = [heads[0] + heads[1], heads[2] + heads[3]]
        total = total + pairs[0] + pairs[1]
        for ref, low in ((k_ref, HD), (v_ref, 2 * HD)):
            ref[:, quad * 128 : (quad + 1) * 128] = jnp.concatenate(
                [pair[:, low : low + HD] for pair in pairs], 1
            )
    gain_ref[...] = total[:, 128:]


def finish_heads(arrived):
    rows = arrived.shape[1]
    return pl.pallas_call(
        finish_kernel,
        out_shape=(
            jax.ShapeDtypeStruct((rows, D), F32),
            jax.ShapeDtypeStruct((rows, D // 2), F32),
            jax.ShapeDtypeStruct((rows, D // 2), F32),
            jax.ShapeDtypeStruct((rows, 128), F32),
        ),
        compiler_params=params(24),
        cost_estimate=cost(1, 2**20),
        name="finish_heads",
    )(arrived)


def finish_kernel_experts(in_ref, up_ref, down_ref, tail_ref):
    many = in_ref.shape[0]
    wide, narrow = up_ref.shape[1] // many, down_ref.shape[1] // many
    for j in range(many):
        up_ref[:, j * wide : (j + 1) * wide] = in_ref[j, :, :wide].astype(F32)
        down_ref[:, j * narrow : (j + 1) * narrow] = in_ref[j, :, wide + 128 :].astype(F32)

    @pl.when(pl.program_id(0) == 0)
    def _():
        tail_ref[...] = jnp.zeros_like(tail_ref)

    for j in range(many):
        tail_ref[...] += in_ref[j, :, wide : wide + 128].astype(F32)


def finish_experts(arrived):
    places, rows, width = arrived.shape
    part = (width - 128) // 3
    return pl.pallas_call(
        finish_kernel_experts,
        out_shape=(
            jax.ShapeDtypeStruct((rows, places * 2 * part), F32),
            jax.ShapeDtypeStruct((rows, places * part), F32),
            jax.ShapeDtypeStruct((rows, 128), F32),
        ),
        grid=(places // 4,),
        in_specs=[pl.BlockSpec((4, rows, width), lambda i: (i, 0, 0))],
        out_specs=(
            pl.BlockSpec((rows, 8 * part), lambda i: (0, i)),
            pl.BlockSpec((rows, 4 * part), lambda i: (0, i)),
            fixed((rows, 128)),
        ),
        compiler_params=params(),
        cost_estimate=cost(1, 5 * 2**20),
        name="finish_experts",
    )(arrived)


def per_device(
    hidden_in,
    out_grad,
    doc_lengths,
    block_order,
    routes,
    attn_norm,
    w_query,
    w_key,
    w_value,
    w_output,
    ffn_norm,
    w_router,
    w_gate_up,
    w_down,
):
    ctx_count = lax.axis_size("ctx")
    ctx_place = lax.axis_index("ctx")
    fsdp_place = lax.axis_index("fsdp")
    copies = ctx_count // E
    own_expert, own_copy = ctx_place // copies, ctx_place % copies
    tok_count = hidden_in.shape[1]
    seq_len = tok_count * ctx_count
    block_len = tok_count // 2
    band = seq_len // 4
    rows = attn_norm.shape[0]
    part = F // copies
    groups = H // KVH
    share = seq_len // copies
    swap_y = [(0, 1), (1, 0)]
    alone = copies == 1

    def swap_fsdp(mine):
        return lax.ppermute(mine, "fsdp", swap_y)

    def both_rows(mine):
        theirs = swap_fsdp(mine)
        stacked = jnp.where(
            fsdp_place == 0, jnp.stack([mine, theirs], 1), jnp.stack([theirs, mine], 1)
        )
        return stacked.reshape(-1, mine.shape[-1])

    def exchange(split):
        return lax.all_to_all(split, "ctx", 0, 0, tiled=True)

    ids = block_order[0]
    block_ids = jnp.arange(ids.shape[0], dtype=jnp.int32)
    spots = jnp.sum(jnp.where(ids[None, :] == block_ids[:, None], block_ids[None, :], 0), axis=1)
    lengths = doc_lengths[0]
    doc_ids = jnp.arange(lengths.shape[0], dtype=jnp.int32)
    firsts = jnp.sum(
        jnp.where(doc_ids[None, :] < doc_ids[:, None], lengths[None, :], 0), axis=1
    )
    tables = tables_of(seq_len)
    order, heads = block_order_of(ctx_count), block_order_of(E)
    where = jnp.stack([own_expert, own_copy, ctx_place, jnp.int32(share)]).astype(jnp.int32)

    def by_expert(weight, pieces):
        split = weight.reshape(rows, E, pieces, copies, part)
        return split.transpose(1, 3, 0, 2, 4).reshape(ctx_count, rows, pieces * part)

    chosen_mask = jnp.any(
        routes[0][:, :, None] == jnp.arange(E, dtype=jnp.int32)[None, None, :], axis=1
    ).astype(BF)
    grads_own = jnp.concatenate(
        [out_grad[0], chosen_mask, jnp.zeros((tok_count, 128 - E), BF)], axis=1
    )
    experts = jnp.concatenate([by_expert(w_gate_up, 2), by_expert(w_down, 1)], axis=2)
    norms = jnp.stack([attn_norm, ffn_norm], 1)
    if alone:
        small_here = exchange(pack_small(copies, w_query, w_key, w_value, w_router, norms))
        w_ext, w_head, router_full, gain_one, gain_two = split_small(both_rows(small_here))
        near = Gather(hidden_in[0])
        near.cross()
        near.last(small_here)
        experts_here = exchange(after(experts, near.two))
        hidden_all = near.join(order, "join_hidden", w_ext).reshape(seq_len, D)
    else:
        small_here = exchange(pack_small(copies, w_query, w_key, w_value, w_router, norms))
        w_ext, w_head, router_full, gain_one, gain_two = split_small(both_rows(small_here))
        hidden_all = lax.all_gather(hidden_in[0], "ctx", axis=0, tiled=True)
        experts_here = exchange(experts)
    out_all = lax.all_gather(w_output, BOTH, axis=0, tiled=True).reshape(ctx_count, 2 * rows, D)
    top_all = lax.all_gather(grads_own[None], "ctx", axis=0, tiled=True)

    heads_all, logs, attended = head_forward(
        hidden_all, w_ext, gain_one, tables, ids, spots, firsts, tok_count, band
    )
    def half_rows(mine, theirs):
        stacked = jnp.where(
            fsdp_place == 0, jnp.stack([mine, theirs], 1), jnp.stack([theirs, mine], 1)
        )
        return stacked.reshape(D, mine.shape[-1])

    if alone:
        att = Gather(attended)
        experts_here = after(experts_here, attended)
    gu_here, dn_here = experts_here[:, :, : 2 * part], experts_here[:, :, 2 * part :]
    gu_there, dn_there = swap_fsdp(gu_here), swap_fsdp(dn_here)
    w_gu, w_dn = half_rows(gu_here, gu_there), half_rows(dn_here, dn_there)
    if alone:
        att.cross()
        att.last(experts_here)
        att_all = att.join(heads, "join_heads", w_gu)
    else:
        sent = lax.dynamic_slice_in_dim(attended, own_copy * share, share, 1)
        att_all = lax.all_gather(sent, "ctx", axis=0, tiled=True)
        att_all = att_all.reshape(H, copies, HD, share).transpose(0, 2, 1, 3)
        att_all = att_all.reshape(H, HD, seq_len)

    mixed, gates, factor, middle = expert_front(
        att_all, hidden_all, out_all, w_gu, gain_two, where, tok_count
    )
    grad_both, act, grad_mid, coef, pull_a, pull_b, norm_sum = expert_back(
        mixed, gates, factor, top_all, out_all, w_gu, w_dn, router_full, gain_two, heads, where,
        tok_count,
    )

    def given_rows(grads):
        by_owner = grads.reshape(ctx_count, 2, rows, grads.shape[1])
        return by_owner, lax.dynamic_index_in_dim(by_owner, 1 - fsdp_place, 1, keepdims=False)

    def to_owner(by_owner, theirs):
        kept = lax.dynamic_index_in_dim(by_owner, fsdp_place, 1, keepdims=False)
        return (kept.astype(F32) + theirs.astype(F32)).astype(BF)

    gu_owner, gu_given = given_rows(up_weights(mixed, grad_both, coef, norm_sum))
    gu_theirs = swap_fsdp(gu_given)
    act_late, act_last = act, act
    if alone:
        ring = RingSum(pull_a, permute(pull_b, SWAP_CORE))
        act_late = after(act, ring.cross_out, gu_given)
    moe = moe_out(act_late, w_dn, tok_count, rows)
    out_both = output_weights(
        att_all, grad_mid, top_all, moe, where, tok_count, rows
    )
    if alone:
        ring.cross()
        out_both = after(out_both, *ring.sends)
        act_last = after(act, *ring.sends)
    dn_owner, dn_given = given_rows(
        down_weights(top_all, act_last, tok_count)
    )
    dn_theirs = swap_fsdp(dn_given)
    if alone:
        upstream = ring.end(dn_given)
        gu_theirs, dn_theirs = after(gu_theirs, upstream), after(dn_theirs, upstream)
    else:
        joined = jnp.concatenate([pull_a, pull_b], 0)
        pulled = lax.psum_scatter(joined, "ctx", scatter_dimension=0, tiled=True)
        rings = [[i * copies + j for j in range(copies)] for i in range(E)]
        pulled = lax.all_gather(pulled, "ctx", axis=0, tiled=True, axis_index_groups=rings)
        own_out = lax.dynamic_slice_in_dim(out_all.reshape(D, D), own_expert * HD, HD, 0)
        top_rows = top_all[:, :, :D].reshape(seq_len, D)
        upstream = pulled.astype(F32) + RESIDUAL_SCALE * dot(own_out, top_rows, 1, 1)
    grads_all_expert = jnp.concatenate(
        [to_owner(gu_owner, gu_theirs), to_owner(dn_owner, dn_theirs)], 2
    )

    own_grads = attend_backward(
        heads_all, upstream, logs, tables, ids, spots, firsts, where, tok_count, band
    )
    own_grads = after(own_grads, grads_all_expert)
    experts_in = exchange(grads_all_expert)
    grad_b, head_sum, norm_head = pull_heads(
        own_grads, w_head, gain_one, hidden_all, grad_mid, jnp.zeros((D, 256), F32),
        jnp.zeros((8, D), F32), order[ctx_count // 2 :], tok_count, False,
    )
    grad_a, grad_heads, ignored = pull_heads(
        own_grads, w_head, gain_one, hidden_all, grad_mid, head_sum, norm_head,
        order[: ctx_count // 2], tok_count, True,
    )
    if alone:
        ring = RingSum(grad_a, permute(grad_b, SWAP_CORE))
        ring.cross()
        experts_in = after(experts_in, *ring.sends)
    else:
        joined = jnp.concatenate([grad_a, grad_b], 0)
        grad_own = lax.psum_scatter(joined, "ctx", scatter_dimension=0, tiled=True).astype(F32)
    def from_experts(block, pieces):
        block = block[:, :, : pieces * part].astype(F32)
        block = block.reshape(E, copies, rows, pieces, part).transpose(2, 0, 3, 1, 4)
        return block.reshape(rows, E * pieces * F)

    if alone:
        share_gate_up, share_down, tail = finish_experts(experts_in)
    else:
        gu_in = experts_in[:, :, : 2 * part + 128]
        dn_in = experts_in[:, :, 2 * part + 128 :]
        share_gate_up = from_experts(gu_in, 2)
        share_down = from_experts(dn_in, 1)
        tail = jnp.sum(gu_in[:, :, 2 * part :].astype(F32), axis=0)
    share_router = tail[:, :E]
    share_gain_two = tail[:, E]
    out_own = lax.psum_scatter(out_both, "ctx", scatter_dimension=0, tiled=False).astype(F32)
    hidden_out = (middle + out_own[:tok_count]).astype(BF)
    out_rows = out_own[tok_count:].reshape(2, rows, D)
    mine = lax.dynamic_index_in_dim(out_rows, fsdp_place, 0, keepdims=False)
    theirs = lax.dynamic_index_in_dim(out_rows, 1 - fsdp_place, 0, keepdims=False)
    share_output = mine + swap_fsdp(theirs)

    if alone:
        grad_own = ring.end(share_output, hidden_out, share_gate_up)
        grad_heads = after(grad_heads, ring.own)
    grad_in = out_grad[0].astype(F32) + grad_own
    tail_in = lax.all_to_all(
        grad_heads.reshape(2 * ctx_count, rows, 256), BOTH, 0, 0, tiled=True
    )
    if alone:
        share_query, share_key, share_value, gain_sum = finish_heads(tail_in)
        share_gain_one = gain_sum[:, HD]
    else:
        tail_in = tail_in.astype(F32).reshape(H, copies * 2, rows, 256)
        heads_in = jnp.sum(tail_in[..., : 3 * HD], axis=1)
        share_query = heads_in[:, :, :HD].transpose(1, 0, 2).reshape(rows, H * HD)
        pairs_in = heads_in[:, :, HD:].reshape(KVH, groups, rows, 2, HD).sum(1)
        share_key = pairs_in[:, :, 0].transpose(1, 0, 2).reshape(rows, KVH * HD)
        share_value = pairs_in[:, :, 1].transpose(1, 0, 2).reshape(rows, KVH * HD)
        share_gain_one = jnp.sum(tail_in[..., 3 * HD], axis=(0, 1))
    return (
        hidden_out[None],
        grad_in[None],
        share_gain_one,
        share_query,
        share_key,
        share_value,
        share_output,
        share_gain_two,
        share_router,
        share_gate_up,
        share_down,
    )


def solution(mesh):
    return jax.shard_map(
        per_device,
        mesh=mesh,
        in_specs=(
            P("fsdp", "ctx", None),
            P("fsdp", "ctx", None),
            P("fsdp", None),
            P("fsdp", None),
            P("fsdp", "ctx", None),
            P(BOTH),
            P(BOTH, None),
            P(BOTH, None),
            P(BOTH, None),
            P(BOTH, None),
            P(BOTH),
            P(BOTH, None),
            P(BOTH, None),
            P(BOTH, None),
        ),
        out_specs=(
            P("fsdp", "ctx", None),
            P("fsdp", "ctx", None),
            P(BOTH),
            P(BOTH, None),
            P(BOTH, None),
            P(BOTH, None),
            P(BOTH, None),
            P(BOTH),
            P(BOTH, None),
            P(BOTH, None),
            P(BOTH, None),
        ),
        check_vma=False,
    )
```

time: 3790 us -> 412 us (0.11)
  waiting for transfers between devices: 3190 us -> 127 us
  local copies, waits for them, and re-layouts: 221 us -> 22.8 us
  matrix products: 188 us -> 0 us
  blocking collectives: 150 us -> 0 us
  Pallas kernels: 0 us -> 145 us
  starting transfers between devices: 0.68 us -> 74.8 us
    reduce_scatter x8 -> x1, waiting for transfers between devices: 2740 us -> 0.01 us  [per_device(): lax.psum_scatter(out_both, 'ctx', scatter_dimension=0, tiled=False)]
    all_gather x8 -> x2, waiting for transfers between devices: 437 us -> 23.9 us  [the longest x1 23.9 us: per_device(): top_all = lax.all_gather(grads_own[None], 'ctx', axis=0, tiled=True)]
    dot_general x37 -> x0, matrix products: 187 us -> none  [the longest x1 24.8 us: per_device(): jnp.einsum('td,tegu->degu', mixed_in, grad_both, preferred_element_type=j...]
    pallas_call x0 -> x16, Pallas kernels: none -> 145 us  [the longest x1 26.8 us: expert_back(): pl.pallas_call(functools.partial(back_kernel, part), out_shape=(out(2 * p...]
    reshape x4, local copies, waits for them, and re-layouts: 108 us -> 2.44 us  [the longest x2 1.34 us: by_expert(): split.transpose(1, 3, 0, 2, 4).reshape(ctx_count, rows, pieces * part)]
    ppermute x0 -> x44, waiting for transfers between devices: none -> 86.6 us  [the longest x38 75 us: permute(): return lax.ppermute(values, 'ctx', pairs)]
    unnamed x2 -> x0, blocking collectives: 82.4 us -> none
    all_gather x1 -> x0, blocking collectives: 67.6 us -> none  [per_device(): lax.all_gather(w_router, ('ctx', 'fsdp'), axis=0, tiled=True)]
  transfers between devices with their start and end apart: 17 -> 51, of which waited for: 15 -> 16; matrix products, arithmetic and copies ran while one was open for 6% -> 11% of each run, Pallas kernels for 0% -> 29%
where the time goes in v1:
time: 412 us; the launch traced here: 410 us
  Pallas kernels  145 us (35%)
  waiting for transfers between devices  127 us (31%)
  starting transfers between devices  74.8 us (18%)
  other arithmetic  26.3 us (6%)
  local copies, waits for them, and re-layouts  22.8 us (6%)
  between operations  14.4 us (3%)
    ppermute x38, waiting for transfers between devices, permute(): return lax.ppermute(values, 'ctx', pairs)  75 us
    ppermute x38, starting transfers between devices, permute(): return lax.ppermute(values, 'ctx', pairs)  45.1 us
    pallas_call x1, Pallas kernels, expert_back(): pl.pallas_call(functools.partial(back_kernel, part), out_shape=(out(2 * p...  26.8 us
    all_gather x1, waiting for transfers between devices, per_device(): top_all = lax.all_gather(grads_own[None], 'ctx', axis=0, tiled=True)  23.9 us
    pallas_call x1, Pallas kernels, head_forward(): pl.pallas_call(functools.partial(head_kernel, count // 2, band), out_shap...  18.4 us
    all_to_all x3, waiting for transfers between devices, exchange(): return lax.all_to_all(split, 'ctx', 0, 0, tiled=True)  16.1 us
    pallas_call x1, Pallas kernels, expert_front(): pl.pallas_call(functools.partial(front_kernel, count), out_shape=(jax.Sha...  15.9 us
    pallas_call x1, Pallas kernels, attend_backward(): pl.pallas_call(functools.partial(attend_kernel, count // 2, band), out_sh...  15.8 us
  transfers between devices with their start and end apart: 51, of which 16 were waited for; matrix products, arithmetic and copies ran while one was open for 11% of the time, Pallas kernels for 29%

profile of v1, /device:TPU:0, one launch (start us, length us, event | category | flops | bytes accessed | tf_op | source)
XLA Modules:
  0.0 410.2 jit_solution(13830849605120415157)
XLA Ops:
  7.2 3.1 collective-permute-start.4
  10.3 2.1 collective-permute-start.5
  15.1 1.8 pack_small.1
  16.9 4.3 %all-to-all-start = ((bf16[16,32,256]{2,1,0:T(8,128)(2,1)}), bf16[16,32,256]{2,1,0:T(8,128)(2,1)S(1)}, u32[]{:S(2)}, u32[]{:S(2)}) async-start(bf16[16,32,256]{2,1,0:T(8,128)(2,1)} %pack_small.1), calls=%async_computation | async-start | bytes 524288 | tf_op jit(solution)/shard_map/all_to_all | solution.py:927
  21.3 2.7 collective-permute-done.5.refs_6_
  25.0 1.6 collective-permute-start.6
  27.8 3.9 all-to-all-done
  31.7 1.5 collective-permute-start.3
  33.2 5.2 %collective-permute-start.7 = (bf16[128,1024]{1,0:T(8,128)(2,1)}, bf16[128,1024]{1,0:T(8,128)(2,1)S(1)}, u32[]{:S(2)}, u32[]{:S(2)}) collective-permute-start(bf16[128,1024]{1,0:T(8,128)(2,1)} %bitcast.95), channel_id=1, source_target_pairs={{0,2},{2,0},{4,6},{6,4},{8,10},{10,8},{12,14},{14,12},{16,18},{18,... | collective-permute-start | bytes 786440 | tf_op jit(solution)/shard_map/ppermute | solution.py:36
  39.2 3.0 collective-permute-done.1.refs_4_
  42.2 1.5 collective-permute-start.2
  48.7 2.4 split_weights.1
  53.6 5.8 %all-to-all-start.1 = ((bf16[16,32,1536]{2,1,0:T(8,128)(2,1)}), bf16[16,32,1536]{2,1,0:T(8,128)(2,1)S(1)}, u32[]{:S(2)}, u32[]{:S(2)}) async-start(bf16[16,32,1536]{2,1,0:T(8,128)(2,1)} %pad_maximum_fusion.1), calls=%async_computation.1 | async-start | bytes 3145728 | tf_op jit(solution)/shard_map/all_to_all | solution.py:927
  60.4 4.9 %join_hidden.1 = bf16[16,128,1024]{2,1,0:T(8,128)(2,1)} custom-call(s32[16]{0:T(128)} %fusion.5.places.heads, bf16[128,1024]{1,0:T(8,128)(2,1)} %bitcast.96, bf16[128,1024]{1,0:T(8,128)(2,1)} %collective-permute-done.refs_1_, bf16[128,1024]{1,0:T(8,128)(2,1)} %copy-done.8, bf16[256,1024]{1,0:T(8,128)(2,1)} %collective-permute-done.6.refs_3_, ...), custom_call_target="tpu_custom_call" | custom-call | flops 20 | bytes 167772160 | tf_op jit(solution)/shard_map/join_hidden/pallas_call | solution.py:132
  65.4 18.4 %head_forward.1 = (bf16[2048,512]{1,0:T(8,128)(2,1)}, f32[2048,1]{1,0:T(8,128)}, bf16[64,2048]{1,0:T(8,128)(2,1)}) custom-call(s32[32]{0:T(128)} %bitcast.109, s32[32]{0:T(128)} %select_reduce_fusion.spots, s32[16]{0:T(128)} %select_reduce_fusion.1.firsts, bf16[2048,1024]{1,0:T(8,128)(2,1)} %bitcast.67, bf16[1024,384]{1,0:T(8,128)(2,1)} %get-tuple-element.61.w_ref, ...), custom_call_target="tpu_custom_call" | custom-call | flops 32212254720 | bytes 83886080 | tf_op jit(solution)/shard_map/head_forward/pallas_call | solution.py:333
  83.8 2.0 collective-permute-start.18
  85.8 1.9 collective-permute-start.19
  87.6 12.1 %all-to-all-done.1 = bf16[16,32,1536]{2,1,0:T(8,128)(2,1)S(1)} async-done(((bf16[16,32,1536]{2,1,0:T(8,128)(2,1)}), bf16[16,32,1536]{2,1,0:T(8,128)(2,1)S(1)}, u32[]{:S(2)}, u32[]{:S(2)}) %all-to-all-start.1) | async-done | bytes 1572896 | tf_op jit(solution)/shard_map/all_to_all | solution.py:927
  101.0 1.5 collective-permute-start.17
  102.5 7.1 %collective-permute-done.19.refs_6_ = bf16[64,2048]{1,0:T(8,128)(2,1)S(1)} collective-permute-done((bf16[64,2048]{1,0:T(8,128)(2,1)}, bf16[64,2048]{1,0:T(8,128)(2,1)S(1)}, u32[]{:S(2)}, u32[]{:S(2)}) %collective-permute-start.19) | collective-permute-done | bytes 262176 | tf_op jit(solution)/shard_map/ppermute | solution.py:36
  109.6 3.6 collective-permute-start.20
  113.3 6.5 %collective-permute-start.15 = (bf16[64,2048]{1,0:T(8,128)(2,1)}, bf16[64,2048]{1,0:T(8,128)(2,1)}, u32[]{:S(2)}, u32[]{:S(2)}) collective-permute-start(bf16[64,2048]{1,0:T(8,128)(2,1)} %get-tuple-element.65.refs_0_), channel_id=1, source_target_pairs={{0,16},{2,18},{4,20},{6,22},{8,24},{10,26},{12,28},{14,30},{16,0},... | collective-permute-start | bytes 786440 | tf_op jit(solution)/shard_map/ppermute | solution.py:36
  120.6 1.5 collective-permute-start.28
  122.1 9.1 %collective-permute-done.15.refs_4_ = bf16[64,2048]{1,0:T(8,128)(2,1)} collective-permute-done((bf16[64,2048]{1,0:T(8,128)(2,1)}, bf16[64,2048]{1,0:T(8,128)(2,1)}, u32[]{:S(2)}, u32[]{:S(2)}) %collective-permute-start.15) | collective-permute-done | bytes 262176 | tf_op jit(solution)/shard_map/ppermute | solution.py:36
  132.0 1.5 collective-permute-start.16
  134.8 1.9 maximum_select_fusion
  136.7 1.5 copy.63
  138.2 2.8 collective-permute-done.16.refs_5_
  145.5 4.9 %join_heads.1.att_ref = bf16[16,64,2048]{2,1,0:T(8,128)(2,1)} custom-call(s32[16]{0:T(128)} %fusion.5.places.heads, bf16[64,2048]{1,0:T(8,128)(2,1)} %get-tuple-element.65.refs_0_, bf16[64,2048]{1,0:T(8,128)(2,1)} %copy-done.17, bf16[64,2048]{1,0:T(8,128)(2,1)} %copy-done.9, bf16[128,2048]{1,0:T(8,128)(2,1)} %collective-permute-done.20.refs_3_, ...), custom_call_target="tpu_custom_call" | custom-call | flops 20 | bytes 167772160 | tf_op jit(solution)/shard_map/join_heads/pallas_call | solution.py:132
  150.4 15.9 %expert_front.1 = (bf16[2048,1024]{1,0:T(8,128)(2,1)}, f32[2048,1024]{1,0:T(8,128)}, f32[2048,128]{1,0:T(8,128)}, f32[128,1024]{1,0:T(8,128)}) custom-call(s32[4]{0:T(128)} %pad_add_fusion.where, bf16[16,64,2048]{2,1,0:T(8,128)(2,1)} %join_heads.1.att_ref, bf16[2048,1024]{1,0:T(8,128)(2,1)} %bitcast.68, bf16[16,64,1024]{2,1,0:T(8,128)(2,1)} %bitcast.104, ...), custom_call_target="tpu_custom_call" | custom-call | flops 171798691840 | bytes 587202560 | tf_op jit(solution)/shard_map/expert_front/pallas_call | solution.py:394
  166.4 23.9 %all-gather.6.cloned.1.call-done = bf16[2048,1152]{1,0:T(8,128)(2,1)} async-done(((bf16[128,1152]{1,0:T(8,128)(2,1)}), bf16[2048,1152]{1,0:T(8,128)(2,1)}) %all-gather.6.cloned.1.call-update) | async-done | bytes 4718608 | tf_op jit(solution)/shard_map/all_gather | solution.py:967
  190.2 26.8 %expert_back.1 = (bf16[2048,1024]{1,0:T(8,128)(2,1)}, bf16[2048,512]{1,0:T(8,128)(2,1)}, bf16[2048,1024]{1,0:T(8,128)(2,1)}, bf16[2048,128]{1,0:T(8,128)(2,1)}, ...) custom-call(s32[16]{0:T(128)} %fusion.5.places.heads, s32[4]{0:T(128)} %pad_add_fusion.where, ...), custom_call_target="tpu_custom_call" | custom-call | flops 214748364800 | bytes 587202560 | tf_op jit(solution)/shard_map/expert_back/pallas_call | solution.py:491
  217.3 10.6 %up_weights.1 = bf16[1024,1152]{1,0:T(8,128)(2,1)} custom-call(bf16[2048,1024]{1,0:T(8,128)(2,1)} %get-tuple-element.73.mixed_ref, bf16[2048,1024]{1,0:T(8,128)(2,1)} %get-tuple-element.81.gb_ref, bf16[2048,128]{1,0:T(8,128)(2,1)} %get-tuple-element.82.coef_ref, f32[8,1024]{1,0:T(8,128)} %get-tuple-element.83.norm_ref), custom_call_target="tpu_custom_call" | custom-call | flops 85899345920 | bytes 167772160 | tf_op jit(solution)/shard_map/up_weights/pallas_call | solution.py:547
  227.9 2.5 dynamic-slice_bitcast_fusion
  230.4 1.5 collective-permute-start.35
  232.9 6.1 %moe_out.1.moe_ref = bf16[16,192,1024]{2,1,0:T(8,128)(2,1)} custom-call(bf16[2048,512]{1,0:T(8,128)(2,1)} %get-tuple-element.87.act_ref, bf16[1024,512]{1,0:T(8,128)(2,1)} %bitcast.82), custom_call_target="tpu_custom_call" | custom-call | flops 42949672960 | bytes 125829120 | tf_op jit(solution)/shard_map/moe_out/pallas_call | solution.py:602
  238.9 10.8 %output_weights.1 = bf16[16,192,1024]{2,1,0:T(8,128)(2,1)} custom-call(s32[4]{0:T(128)} %pad_add_fusion.where, bf16[16,64,2048]{2,1,0:T(8,128)(2,1)} %join_heads.1.att_ref, bf16[2048,1024]{1,0:T(8,128)(2,1)} %get-tuple-element.77.v_ref.gm_ref.hm_ref, bf16[16,128,1152]{2,1,0:T(8,128)(2,1)} %bitcast.102, ...), custom_call_target="tpu_custom_call", output_to_operand_aliasing={{}: (4, {})} | custom-call | flops 85899345920 | bytes 335544320 | tf_op jit(solution)/shard_map/output_weights/pallas_call | solution.py:638
  249.8 2.1 collective-permute-done.30
  251.8 2.7 add_convert_fusion.8
  254.5 1.5 collective-permute-start.34
  256.0 2.3 collective-permute-start.33
  259.0 6.4 %down_weights.1 = bf16[1024,512]{1,0:T(8,128)(2,1)} custom-call(bf16[16,128,1152]{2,1,0:T(8,128)(2,1)} %bitcast.103, bf16[2048,512]{1,0:T(8,128)(2,1)} %get-tuple-element.87.act_ref), custom_call_target="tpu_custom_call" | custom-call | flops 42949672960 | bytes 125829120 | tf_op jit(solution)/shard_map/down_weights/pallas_call | solution.py:579
  266.8 13.5 %collective-permute-done.32 = bf16[64,2048]{1,0:T(8,128)(2,1)S(1)} collective-permute-done((bf16[64,2048]{1,0:T(8,128)(2,1)}, bf16[64,2048]{1,0:T(8,128)(2,1)S(1)}, u32[]{:S(2)}, u32[]{:S(2)}) %collective-permute-start.32) | collective-permute-done | bytes 262176 | tf_op jit(solution)/shard_map/ppermute | solution.py:36
  280.8 1.9 convert_add_fusion.2.up_ref
  282.8 1.7 fusion
  284.4 9.2 %collective-permute-done.36 = bf16[16,32,512]{2,1,0:T(8,128)(2,1)S(1)} collective-permute-done((bf16[16,32,512]{2,1,0:T(8,128)(2,1)S(1)}, bf16[16,32,512]{2,1,0:T(8,128)(2,1)S(1)}, u32[]{:S(2)}, u32[]{:S(2)}) %collective-permute-start.36) | collective-permute-done | bytes 524320 | tf_op jit(solution)/shard_map/ppermute | solution.py:917
  293.8 1.4 pad_maximum_fusion
  295.2 3.7 all-to-all-start.2
  298.9 15.8 %attend_backward.1.g_ref.h_ref = bf16[2048,256]{1,0:T(8,128)(2,1)} custom-call(s32[32]{0:T(128)} %bitcast.110, s32[32]{0:T(128)} %select_reduce_fusion.spots, s32[16]{0:T(128)} %select_reduce_fusion.1.firsts, s32[4]{0:T(128)} %pad_add_fusion.where, bf16[2048,512]{1,0:T(8,128)(2,1)} %get-tuple-element.86.all_ref, f32[64,2048]{1,0:T(8,128)} %convert_add_fusion.2.up_ref, ...), custom_call_target="tpu_custom_call" | custom-call | flops 40265318400 | bytes 83886080 | tf_op jit(solution)/shard_map/attend_backward/pallas_call | solution.py:715
  316.4 7.9 %pull_first.1 = (bf16[1024,1024]{1,0:T(8,128)(2,1)}, f32[1024,256]{1,0:T(8,128)}, f32[8,1024]{1,0:T(8,128)}) custom-call(s32[8]{0:T(128)} %get-tuple-element.172.order, bf16[2048,256]{1,0:T(8,128)(2,1)} %attend_backward.1.g_ref.h_ref, bf16[2048,256]{1,0:T(8,128)(2,1)} %attend_backward.1.g_ref.h_ref, bf16[1024,256]{1,0:T(8,128)(2,1)} %get-tuple-element.93.w_ref, ...), custom_call_target="tpu_custom_call" | custom-call | flops 1073741824 | bytes 6291456 | tf_op jit(solution)/shard_map/pull_first/pallas_call | solution.py:783
  324.7 7.8 %pull_last.1 = (bf16[1024,1024]{1,0:T(8,128)(2,1)}, bf16[1024,256]{1,0:T(8,128)(2,1)}, f32[8,1024]{1,0:T(8,128)}) custom-call(s32[8]{0:T(128)} %get-tuple-element.171.order, bf16[2048,256]{1,0:T(8,128)(2,1)} %attend_backward.1.g_ref.h_ref, bf16[2048,256]{1,0:T(8,128)(2,1)} %attend_backward.1.g_ref.h_ref, bf16[1024,256]{1,0:T(8,128)(2,1)} %get-tuple-element.93.w_ref, ...), custom_call_target="tpu_custom_call" | custom-call | flops 1073741824 | bytes 6291456 | tf_op jit(solution)/shard_map/pull_last/pallas_call | solution.py:783
  332.5 2.4 add_convert_fusion.6
  334.9 1.6 collective-permute-start.38
  337.1 11.6 %collective-permute-done.38 = bf16[128,1024]{1,0:T(8,128)(2,1)S(1)} collective-permute-done((bf16[128,1024]{1,0:T(8,128)(2,1)S(1)}, bf16[128,1024]{1,0:T(8,128)(2,1)S(1)}, u32[]{:S(2)}, u32[]{:S(2)}) %collective-permute-start.38) | collective-permute-done | bytes 262176 | tf_op jit(solution)/shard_map/ppermute | solution.py:36
  348.7 8.5 %all-to-all-start.3 = ((bf16[32,32,256]{2,1,0:T(8,128)(2,1)}), bf16[32,32,256]{2,1,0:T(8,128)(2,1)S(1)}, u32[]{:S(2)}, u32[]{:S(2)}) async-start(bf16[32,32,256]{2,1,0:T(8,128)(2,1)} %bitcast.35), calls=%async_computation.4 | async-start | bytes 1048576 | tf_op jit(solution)/shard_map/all_to_all | solution.py:1089
  357.2 15.4 %collective-permute-done.39 = bf16[384,1024]{1,0:T(8,128)(2,1)} collective-permute-done((bf16[384,1024]{1,0:T(8,128)(2,1)S(1)}, bf16[384,1024]{1,0:T(8,128)(2,1)}, u32[]{:S(2)}, u32[]{:S(2)}) %collective-permute-start.39) | collective-permute-done | bytes 786464 | tf_op jit(solution)/shard_map/ppermute | solution.py:36
  372.6 2.7 add_convert_fusion.2
  376.6 2.6 collective-permute-start.42
  379.2 4.0 finish_experts.1
  383.1 1.4 copy.67
  384.5 1.4 slice_reduce_fusion
  391.0 2.4 collective-permute-done.41
  394.1 7.4 %collective-permute-done.40 = bf16[128,1024]{1,0:T(8,128)(2,1)S(1)} collective-permute-done((bf16[128,1024]{1,0:T(8,128)(2,1)}, bf16[128,1024]{1,0:T(8,128)(2,1)S(1)}, u32[]{:S(2)}, u32[]{:S(2)}) %collective-permute-start.40) | collective-permute-done | bytes 262176 | tf_op jit(solution)/shard_map/ppermute | solution.py:36
  401.5 2.1 add_bitcast_fusion
  (176 shorter events, 36.4 us)
Async XLA Ops:
  7.2 31.4 %copy-start.32 = (s32[1,16]{1,0:T(1,128)S(1)}, s32[1,16]{1,0:T(1,128)}, u32[]{:S(2)}) copy-start(s32[1,16]{1,0:T(1,128)} %param.18) | copy-start | bytes 196
  7.2 37.2 %copy-start.14 = (bf16[32,8192]{1,0:T(8,128)(2,1)S(1)}, bf16[32,8192]{1,0:T(8,128)(2,1)}, u32[]{:S(2)}) copy-start(bf16[32,8192]{1,0:T(8,128)(2,1)} %param.29) | copy-start | bytes 1572868
  7.2 14.1 %collective-permute-start.4 = (bf16[128,1024]{1,0:T(8,128)(2,1)}, bf16[128,1024]{1,0:T(8,128)(2,1)S(1)}, u32[]{:S(2)}, u32[]{:S(2)}) collective-permute-start(bf16[128,1024]{1,0:T(8,128)(2,1)} %bitcast.91), channel_id=1, source_target_pairs={{0,8},{2,10},{4,12},{6,14},{8,16},{10,18},{12,20},{14,22},{16,24},... | collective-permute-start | bytes 786440 | tf_op jit(solution)/shard_map/ppermute | solution.py:36
  10.3 13.7 %collective-permute-start.5 = (bf16[128,1024]{1,0:T(8,128)(2,1)}, bf16[128,1024]{1,0:T(8,128)(2,1)}, u32[]{:S(2)}, u32[]{:S(2)}) collective-permute-start(bf16[128,1024]{1,0:T(8,128)(2,1)} %bitcast.92), channel_id=1, source_target_pairs={{0,24},{2,26},{4,28},{6,30},{8,0},{10,2},{12,4},{14,6},{16,8},{18,... | collective-permute-start | bytes 786440 | tf_op jit(solution)/shard_map/ppermute | solution.py:36
  15.1 29.8 %copy-start.7 = (bf16[32,16384]{1,0:T(8,128)(2,1)S(1)}, bf16[32,16384]{1,0:T(8,128)(2,1)}, u32[]{:S(2)}) copy-start(bf16[32,16384]{1,0:T(8,128)(2,1)} %param.28) | copy-start | bytes 3145732
  16.9 14.8 %all-to-all-start = ((bf16[16,32,256]{2,1,0:T(8,128)(2,1)}), bf16[16,32,256]{2,1,0:T(8,128)(2,1)S(1)}, u32[]{:S(2)}, u32[]{:S(2)}) async-start(bf16[16,32,256]{2,1,0:T(8,128)(2,1)} %pack_small.1), calls=%async_computation | async-start | bytes 524288 | tf_op jit(solution)/shard_map/all_to_all | solution.py:927
  21.2 129.2 %all-gather.4.cloned.1.call-start = ((), (), s32[]{:S(2)}) async-start(), calls=%async_computation.5 | async-start | bytes 2162688 | tf_op jit(solution)/shard_map/all_gather | solution.py:966
  21.3 24.5 %copy-start.8 = (bf16[128,1024]{1,0:T(8,128)(2,1)}, bf16[128,1024]{1,0:T(8,128)(2,1)S(1)}, u32[]{:S(2)}) copy-start(bf16[128,1024]{1,0:T(8,128)(2,1)S(1)} %collective-permute-done.4.refs_2_) | copy-start | bytes 786436
  25.0 18.8 %collective-permute-start.6 = (bf16[256,1024]{1,0:T(8,128)(2,1)S(1)}, bf16[256,1024]{1,0:T(8,128)(2,1)}, u32[]{:S(2)}, u32[]{:S(2)}) collective-permute-start(bf16[256,1024]{1,0:T(8,128)(2,1)S(1)} %pad_maximum_fusion.4), channel_id=1, source_target_pairs={{0,4},{2,6},{4,0},{6,2},{8,12},{10,14},{12,8},{14,10},{16,20},{18,... | collective-permute-start | bytes 1572872 | tf_op jit(solution)/shard_map/ppermute | solution.py:36
  26.5 15.7 %collective-permute-start.1 = (bf16[128,1024]{1,0:T(8,128)(2,1)}, bf16[128,1024]{1,0:T(8,128)(2,1)}, u32[]{:S(2)}, u32[]{:S(2)}) collective-permute-start(bf16[128,1024]{1,0:T(8,128)(2,1)} %bitcast.93), channel_id=1, source_target_pairs={{0,16},{2,18},{4,20},{6,22},{8,24},{10,26},{12,28},{14,30},{16,0},... | collective-permute-start | bytes 786440 | tf_op jit(solution)/shard_map/ppermute | solution.py:36
  31.7 10.5 %collective-permute-start.3 = (bf16[16,32,256]{2,1,0:T(8,128)(2,1)S(1)}, bf16[16,32,256]{2,1,0:T(8,128)(2,1)S(1)}, u32[]{:S(2)}, u32[]{:S(2)}) collective-permute-start(bf16[16,32,256]{2,1,0:T(8,128)(2,1)S(1)} %all-to-all-done), channel_id=1, source_target_pairs={{0,1},{1,0},{2,3},{3,2},{4,5},{5,4},{6,7},{7,6},{8,9},{9,8},{10,11... | collective-permute-start | bytes 786440 | tf_op jit(solution)/shard_map/ppermute | solution.py:917
  33.2 17.8 %collective-permute-start = (bf16[128,1024]{1,0:T(8,128)(2,1)}, bf16[128,1024]{1,0:T(8,128)(2,1)}, u32[]{:S(2)}, u32[]{:S(2)}) collective-permute-start(bf16[128,1024]{1,0:T(8,128)(2,1)} %bitcast.94), channel_id=1, source_target_pairs={{0,4},{2,6},{4,0},{6,2},{8,12},{10,14},{12,8},{14,10},{16,20},{18,... | collective-permute-start | bytes 786440 | tf_op jit(solution)/shard_map/ppermute | solution.py:36
  33.2 18.5 %collective-permute-start.7 = (bf16[128,1024]{1,0:T(8,128)(2,1)}, bf16[128,1024]{1,0:T(8,128)(2,1)S(1)}, u32[]{:S(2)}, u32[]{:S(2)}) collective-permute-start(bf16[128,1024]{1,0:T(8,128)(2,1)} %bitcast.95), channel_id=1, source_target_pairs={{0,2},{2,0},{4,6},{6,4},{8,10},{10,8},{12,14},{14,12},{16,18},{18,... | collective-permute-start | bytes 786440 | tf_op jit(solution)/shard_map/ppermute | solution.py:36
  42.2 10.0 %collective-permute-start.9 = (bf16[128,1024]{1,0:T(8,128)(2,1)S(1)}, bf16[128,1024]{1,0:T(8,128)(2,1)}, u32[]{:S(2)}, u32[]{:S(2)}) collective-permute-start(bf16[128,1024]{1,0:T(8,128)(2,1)S(1)} %collective-permute-done.4.refs_2_), channel_id=1, source_target_pairs={{0,2},{2,0},{4,6},{6,4},{8,10},{10,8},{12,14},{14,12},{16,18},{18,... | collective-permute-start | bytes 786440 | tf_op jit(solution)/shard_map/ppermute | solution.py:36
  42.2 9.5 %collective-permute-start.2 = (bf16[128,1024]{1,0:T(8,128)(2,1)}, bf16[128,1024]{1,0:T(8,128)(2,1)}, u32[]{:S(2)}, u32[]{:S(2)}) collective-permute-start(bf16[128,1024]{1,0:T(8,128)(2,1)} %collective-permute-done.1.refs_4_), channel_id=1, source_target_pairs={{0,4},{2,6},{4,0},{6,2},{8,12},{10,14},{12,8},{14,10},{16,20},{18,... | collective-permute-start | bytes 786440 | tf_op jit(solution)/shard_map/ppermute | solution.py:36
  43.7 15.8 %collective-permute-start.10 = (bf16[256,1024]{1,0:T(8,128)(2,1)}, bf16[256,1024]{1,0:T(8,128)(2,1)}, u32[]{:S(2)}, u32[]{:S(2)}) collective-permute-start(bf16[256,1024]{1,0:T(8,128)(2,1)} %collective-permute-done.6.refs_3_), channel_id=1, source_target_pairs={{0,2},{2,0},{4,6},{6,4},{8,10},{10,8},{12,14},{14,12},{16,18},{18,... | collective-permute-start | bytes 1572872 | tf_op jit(solution)/shard_map/ppermute | solution.py:36
  51.1 8.4 %collective-permute-start.13 = (bf16[128,1024]{1,0:T(8,128)(2,1)}, bf16[128,1024]{1,0:T(8,128)(2,1)S(1)}, u32[]{:S(2)}, u32[]{:S(2)}) collective-permute-start(bf16[128,1024]{1,0:T(8,128)(2,1)} %collective-permute-done.5.refs_6_), channel_id=1, source_target_pairs={{0,2},{2,0},{4,6},{6,4},{8,10},{10,8},{12,14},{14,12},{16,18},{18,... | collective-permute-start | bytes 786440 | tf_op jit(solution)/shard_map/ppermute | solution.py:36
  51.7 7.8 %collective-permute-start.11 = (bf16[128,1024]{1,0:T(8,128)(2,1)}, bf16[128,1024]{1,0:T(8,128)(2,1)S(1)}, u32[]{:S(2)}, u32[]{:S(2)}) collective-permute-start(bf16[128,1024]{1,0:T(8,128)(2,1)} %collective-permute-done.1.refs_4_), channel_id=1, source_target_pairs={{0,2},{2,0},{4,6},{6,4},{8,10},{10,8},{12,14},{14,12},{16,18},{18,... | collective-permute-start | bytes 786440 | tf_op jit(solution)/shard_map/ppermute | solution.py:36
  51.7 7.8 %collective-permute-start.8 = (bf16[128,1024]{1,0:T(8,128)(2,1)}, bf16[128,1024]{1,0:T(8,128)(2,1)S(1)}, u32[]{:S(2)}, u32[]{:S(2)}) collective-permute-start(bf16[128,1024]{1,0:T(8,128)(2,1)} %collective-permute-done.refs_1_), channel_id=1, source_target_pairs={{0,2},{2,0},{4,6},{6,4},{8,10},{10,8},{12,14},{14,12},{16,18},{18,... | collective-permute-start | bytes 786440 | tf_op jit(solution)/shard_map/ppermute | solution.py:36
  52.2 7.3 %collective-permute-start.12 = (bf16[128,1024]{1,0:T(8,128)(2,1)}, bf16[128,1024]{1,0:T(8,128)(2,1)S(1)}, u32[]{:S(2)}, u32[]{:S(2)}) collective-permute-start(bf16[128,1024]{1,0:T(8,128)(2,1)} %collective-permute-done.2.refs_5_), channel_id=1, source_target_pairs={{0,2},{2,0},{4,6},{6,4},{8,10},{10,8},{12,14},{14,12},{16,18},{18,... | collective-permute-start | bytes 786440 | tf_op jit(solution)/shard_map/ppermute | solution.py:36
  53.6 46.2 %all-to-all-start.1 = ((bf16[16,32,1536]{2,1,0:T(8,128)(2,1)}), bf16[16,32,1536]{2,1,0:T(8,128)(2,1)S(1)}, u32[]{:S(2)}, u32[]{:S(2)}) async-start(bf16[16,32,1536]{2,1,0:T(8,128)(2,1)} %pad_maximum_fusion.1), calls=%async_computation.1 | async-start | bytes 3145728 | tf_op jit(solution)/shard_map/all_to_all | solution.py:927
  59.4 130.8 %all-gather.6.cloned.1.call-start = ((), (), s32[]{:S(2)}) async-start(), calls=%async_computation.7 | async-start | bytes 5013504 | tf_op jit(solution)/shard_map/all_gather | solution.py:967
  83.8 18.7 %collective-permute-start.18 = (bf16[64,2048]{1,0:T(8,128)(2,1)}, bf16[64,2048]{1,0:T(8,128)(2,1)S(1)}, u32[]{:S(2)}, u32[]{:S(2)}) collective-permute-start(bf16[64,2048]{1,0:T(8,128)(2,1)} %get-tuple-element.65.refs_0_), channel_id=1, source_target_pairs={{0,8},{2,10},{4,12},{6,14},{8,16},{10,18},{12,20},{14,22},{16,24},... | collective-permute-start | bytes 786440 | tf_op jit(solution)/shard_map/ppermute | solution.py:36
  85.8 23.8 %collective-permute-start.19 = (bf16[64,2048]{1,0:T(8,128)(2,1)}, bf16[64,2048]{1,0:T(8,128)(2,1)S(1)}, u32[]{:S(2)}, u32[]{:S(2)}) collective-permute-start(bf16[64,2048]{1,0:T(8,128)(2,1)} %get-tuple-element.65.refs_0_), channel_id=1, source_target_pairs={{0,24},{2,26},{4,28},{6,30},{8,0},{10,2},{12,4},{14,6},{16,8},{18,... | collective-permute-start | bytes 786440 | tf_op jit(solution)/shard_map/ppermute | solution.py:36
  101.0 32.4 %copy-start.31 = (s32[1,128,8]{1,2,0:T(8,128)S(1)}, s32[1,128,8]{1,2,0:T(8,128)}, u32[]{:S(2)}) copy-start(s32[1,128,8]{1,2,0:T(8,128)} %param.20) | copy-start | bytes 12292
  101.0 32.6 %copy-start.5 = (bf16[1,128,1024]{2,1,0:T(8,128)(2,1)S(1)}, bf16[1,128,1024]{2,1,0:T(8,128)(2,1)}, u32[]{:S(2)}) copy-start(bf16[1,128,1024]{2,1,0:T(8,128)(2,1)} %param.17) | copy-start | bytes 786436
  101.0 33.5 %collective-permute-start.17 = (bf16[16,32,1024]{2,1,0:T(8,128)(2,1)}, bf16[16,32,1024]{2,1,0:T(8,128)(2,1)}, u32[]{:S(2)}, u32[]{:S(2)}) collective-permute-start(bf16[16,32,1024]{2,1,0:T(8,128)(2,1)} %get-tuple-element.170), channel_id=1, source_target_pairs={{0,1},{1,0},{2,3},{3,2},{4,5},{5,4},{6,7},{7,6},{8,9},{9,8},{10,11... | collective-permute-start | bytes 3145736 | tf_op jit(solution)/shard_map/ppermute | solution.py:917
  102.5 10.8 %copy-start.9 = (bf16[64,2048]{1,0:T(8,128)(2,1)}, bf16[64,2048]{1,0:T(8,128)(2,1)S(1)}, u32[]{:S(2)}) copy-start(bf16[64,2048]{1,0:T(8,128)(2,1)S(1)} %collective-permute-done.18.refs_2_) | copy-start | bytes 786436
  109.6 22.2 %collective-permute-start.20 = (bf16[128,2048]{1,0:T(8,128)(2,1)S(1)}, bf16[128,2048]{1,0:T(8,128)(2,1)}, u32[]{:S(2)}, u32[]{:S(2)}) collective-permute-start(bf16[128,2048]{1,0:T(8,128)(2,1)S(1)} %pad_maximum_fusion.5), channel_id=1, source_target_pairs={{0,4},{2,6},{4,0},{6,2},{8,12},{10,14},{12,8},{14,10},{16,20},{18,... | collective-permute-start | bytes 1572872 | tf_op jit(solution)/shard_map/ppermute | solution.py:36
  113.2 18.1 %collective-permute-start.14 = (bf16[64,2048]{1,0:T(8,128)(2,1)}, bf16[64,2048]{1,0:T(8,128)(2,1)S(1)}, u32[]{:S(2)}, u32[]{:S(2)}) collective-permute-start(bf16[64,2048]{1,0:T(8,128)(2,1)} %get-tuple-element.65.refs_0_), channel_id=1, source_target_pairs={{0,4},{2,6},{4,0},{6,2},{8,12},{10,14},{12,8},{14,10},{16,20},{18,... | collective-permute-start | bytes 786440 | tf_op jit(solution)/shard_map/ppermute | solution.py:36
  113.3 18.0 %collective-permute-start.15 = (bf16[64,2048]{1,0:T(8,128)(2,1)}, bf16[64,2048]{1,0:T(8,128)(2,1)}, u32[]{:S(2)}, u32[]{:S(2)}) collective-permute-start(bf16[64,2048]{1,0:T(8,128)(2,1)} %get-tuple-element.65.refs_0_), channel_id=1, source_target_pairs={{0,16},{2,18},{4,20},{6,22},{8,24},{10,26},{12,28},{14,30},{16,0},... | collective-permute-start | bytes 786440 | tf_op jit(solution)/shard_map/ppermute | solution.py:36
  120.6 21.0 %collective-permute-start.28 = (bf16[16,32,512]{2,1,0:T(8,128)(2,1)}, bf16[16,32,512]{2,1,0:T(8,128)(2,1)S(1)}, u32[]{:S(2)}, u32[]{:S(2)}) collective-permute-start(bf16[16,32,512]{2,1,0:T(8,128)(2,1)} %get-tuple-element.168), channel_id=1, source_target_pairs={{0,1},{1,0},{2,3},{3,2},{4,5},{5,4},{6,7},{7,6},{8,9},{9,8},{10,11... | collective-permute-start | bytes 1572872 | tf_op jit(solution)/shard_map/ppermute | solution.py:917
  131.2 9.8 %collective-permute-start.21 = (bf16[64,2048]{1,0:T(8,128)(2,1)}, bf16[64,2048]{1,0:T(8,128)(2,1)S(1)}, u32[]{:S(2)}, u32[]{:S(2)}) collective-permute-start(bf16[64,2048]{1,0:T(8,128)(2,1)} %get-tuple-element.65.refs_0_), channel_id=1, source_target_pairs={{0,2},{2,0},{4,6},{6,4},{8,10},{10,8},{12,14},{14,12},{16,18},{18,... | collective-permute-start | bytes 786440 | tf_op jit(solution)/shard_map/ppermute | solution.py:36
  131.2 10.3 %collective-permute-start.23 = (bf16[64,2048]{1,0:T(8,128)(2,1)}, bf16[64,2048]{1,0:T(8,128)(2,1)S(1)}, u32[]{:S(2)}, u32[]{:S(2)}) collective-permute-start(bf16[64,2048]{1,0:T(8,128)(2,1)} %copy-done.9), channel_id=1, source_target_pairs={{0,2},{2,0},{4,6},{6,4},{8,10},{10,8},{12,14},{14,12},{16,18},{18,... | collective-permute-start | bytes 786440 | tf_op jit(solution)/shard_map/ppermute | solution.py:36
  132.0 9.0 %collective-permute-start.16 = (bf16[64,2048]{1,0:T(8,128)(2,1)}, bf16[64,2048]{1,0:T(8,128)(2,1)}, u32[]{:S(2)}, u32[]{:S(2)}) collective-permute-start(bf16[64,2048]{1,0:T(8,128)(2,1)} %collective-permute-done.15.refs_4_), channel_id=1, source_target_pairs={{0,4},{2,6},{4,0},{6,2},{8,12},{10,14},{12,8},{14,10},{16,20},{18,... | collective-permute-start | bytes 786440 | tf_op jit(solution)/shard_map/ppermute | solution.py:36
  134.4 253.0 %reduce-scatter.2.cloned.1.call-start = ((), (), s32[]{:S(2)}) async-start(), calls=%async_computation.6 | async-start | bytes 6684672 | tf_op jit(solution)/shard_map/reduce_scatter | solution.py:1078
  134.5 9.9 %collective-permute-start.24 = (bf16[128,2048]{1,0:T(8,128)(2,1)}, bf16[128,2048]{1,0:T(8,128)(2,1)S(1)}, u32[]{:S(2)}, u32[]{:S(2)}) collective-permute-start(bf16[128,2048]{1,0:T(8,128)(2,1)} %collective-permute-done.20.refs_3_), channel_id=1, source_target_pairs={{0,2},{2,0},{4,6},{6,4},{8,10},{10,8},{12,14},{14,12},{16,18},{18,... | collective-permute-start | bytes 1572872 | tf_op jit(solution)/shard_map/ppermute | solution.py:36
  141.0 3.4 collective-permute-start.27
  141.0 3.4 collective-permute-start.25
  141.5 3.0 collective-permute-start.22
  141.7 2.8 collective-permute-start.26
  217.0 14.9 %collective-permute-start.29 = (bf16[512,2048]{1,0:T(8,128)(2,1)}, bf16[512,2048]{1,0:T(8,128)(2,1)S(1)}, u32[]{:S(2)}, u32[]{:S(2)}) collective-permute-start(bf16[512,2048]{1,0:T(8,128)(2,1)} %get-tuple-element.80), channel_id=1, source_target_pairs={{0,2},{2,0},{4,6},{6,4},{8,10},{10,8},{12,14},{14,12},{16,18},{18,... | collective-permute-start | bytes 6291464 | tf_op jit(solution)/shard_map/ppermute | solution.py:36
  230.4 52.3 %collective-permute-start.35 = (bf16[16,32,1152]{2,1,0:T(8,128)(2,1)}, bf16[16,32,1152]{2,1,0:T(8,128)(2,1)}, u32[]{:S(2)}, u32[]{:S(2)}) collective-permute-start(bf16[16,32,1152]{2,1,0:T(8,128)(2,1)} %dynamic-slice_bitcast_fusion), channel_id=1, source_target_pairs={{0,1},{1,0},{2,3},{3,2},{4,5},{5,4},{6,7},{7,6},{8,9},{9,8},{10,11... | collective-permute-start | bytes 3538952 | tf_op jit(solution)/shard_map/ppermute | solution.py:917
  231.9 7.0 %copy-start.4 = (bf16[512,2048]{1,0:T(8,128)(2,1)}, bf16[512,2048]{1,0:T(8,128)(2,1)S(1)}, u32[]{:S(2)}) copy-start(bf16[512,2048]{1,0:T(8,128)(2,1)S(1)} %collective-permute-done.29) | copy-start | bytes 6291460
  232.2 19.6 %collective-permute-start.30 = (bf16[192,2048]{1,0:T(8,128)(2,1)S(1)}, bf16[192,2048]{1,0:T(8,128)(2,1)}, u32[]{:S(2)}, u32[]{:S(2)}) collective-permute-start(bf16[192,2048]{1,0:T(8,128)(2,1)S(1)} %pad_maximum_fusion.2), channel_id=1, source_target_pairs={{0,4},{2,6},{4,0},{6,2},{8,12},{10,14},{12,8},{14,10},{16,20},{18,... | collective-permute-start | bytes 2359304 | tf_op jit(solution)/shard_map/ppermute | solution.py:36
  254.5 26.3 %collective-permute-start.34 = (bf16[64,2048]{1,0:T(8,128)(2,1)}, bf16[64,2048]{1,0:T(8,128)(2,1)S(1)}, u32[]{:S(2)}, u32[]{:S(2)}) collective-permute-start(bf16[64,2048]{1,0:T(8,128)(2,1)} %get-tuple-element.156), channel_id=1, source_target_pairs={{0,8},{2,10},{4,12},{6,14},{8,16},{10,18},{12,20},{14,22},{16,24},... | collective-permute-start | bytes 786440 | tf_op jit(solution)/shard_map/ppermute | solution.py:36
  256.0 24.8 %collective-permute-start.33 = (bf16[64,2048]{1,0:T(8,128)(2,1)S(1)}, bf16[64,2048]{1,0:T(8,128)(2,1)S(1)}, u32[]{:S(2)}, u32[]{:S(2)}) collective-permute-start(bf16[64,2048]{1,0:T(8,128)(2,1)S(1)} %get-tuple-element.157), channel_id=1, source_target_pairs={{0,24},{2,26},{4,28},{6,30},{8,0},{10,2},{12,4},{14,6},{16,8},{18,... | collective-permute-start | bytes 786440 | tf_op jit(solution)/shard_map/ppermute | solution.py:36
  258.3 21.9 %collective-permute-start.32 = (bf16[64,2048]{1,0:T(8,128)(2,1)}, bf16[64,2048]{1,0:T(8,128)(2,1)S(1)}, u32[]{:S(2)}, u32[]{:S(2)}) collective-permute-start(bf16[64,2048]{1,0:T(8,128)(2,1)} %get-tuple-element.158), channel_id=1, source_target_pairs={{0,16},{2,18},{4,20},{6,22},{8,24},{10,26},{12,28},{14,30},{16,0},... | collective-permute-start | bytes 786440 | tf_op jit(solution)/shard_map/ppermute | solution.py:36
  258.4 22.4 %collective-permute-start.31 = (bf16[64,2048]{1,0:T(8,128)(2,1)S(1)}, bf16[64,2048]{1,0:T(8,128)(2,1)S(1)}, u32[]{:S(2)}, u32[]{:S(2)}) collective-permute-start(bf16[64,2048]{1,0:T(8,128)(2,1)S(1)} %get-tuple-element.163), channel_id=1, source_target_pairs={{0,4},{2,6},{4,0},{6,2},{8,12},{10,14},{12,8},{14,10},{16,20},{18,... | collective-permute-start | bytes 786440 | tf_op jit(solution)/shard_map/ppermute | solution.py:36
  265.5 17.3 %copy-start.1 = (bf16[1024,1152]{1,0:T(8,128)(2,1)S(1)}, bf16[1024,1152]{1,0:T(8,128)(2,1)}, u32[]{:S(2)}) copy-start(bf16[1024,1152]{1,0:T(8,128)(2,1)} %up_weights.1) | copy-start | bytes 7077892
  280.3 13.3 %collective-permute-start.36 = (bf16[16,32,512]{2,1,0:T(8,128)(2,1)S(1)}, bf16[16,32,512]{2,1,0:T(8,128)(2,1)S(1)}, u32[]{:S(2)}, u32[]{:S(2)}) collective-permute-start(bf16[16,32,512]{2,1,0:T(8,128)(2,1)S(1)} %dynamic-slice_bitcast_fusion.1), channel_id=1, source_target_pairs={{0,1},{1,0},{2,3},{3,2},{4,5},{5,4},{6,7},{7,6},{8,9},{9,8},{10,11... | collective-permute-start | bytes 1572872 | tf_op jit(solution)/shard_map/ppermute | solution.py:917
  282.8 10.8 %copy-start.12 = (bf16[1024,512]{1,0:T(8,128)(2,1)S(1)}, bf16[1024,512]{1,0:T(8,128)(2,1)}, u32[]{:S(2)}) copy-start(bf16[1024,512]{1,0:T(8,128)(2,1)} %down_weights.1) | copy-start | bytes 3145732
  295.2 53.5 %all-to-all-start.2 = ((bf16[16,32,1664]{2,1,0:T(8,128)(2,1)}), bf16[16,32,1664]{2,1,0:T(8,128)(2,1)S(1)}, u32[]{:S(2)}, u32[]{:S(2)}) async-start(bf16[16,32,1664]{2,1,0:T(8,128)(2,1)} %pad_maximum_fusion), calls=%async_computation.3 | async-start | bytes 3407872 | tf_op jit(solution)/shard_map/all_to_all | solution.py:927
  324.2 8.3 %collective-permute-start.37 = (bf16[1024,1024]{1,0:T(8,128)(2,1)}, bf16[1024,1024]{1,0:T(8,128)(2,1)S(1)}, u32[]{:S(2)}, u32[]{:S(2)}) collective-permute-start(bf16[1024,1024]{1,0:T(8,128)(2,1)} %get-tuple-element.97), channel_id=1, source_target_pairs={{0,2},{2,0},{4,6},{6,4},{8,10},{10,8},{12,14},{14,12},{16,18},{18,... | collective-permute-start | bytes 6291464 | tf_op jit(solution)/shard_map/ppermute | solution.py:36
  334.9 13.8 %collective-permute-start.38 = (bf16[128,1024]{1,0:T(8,128)(2,1)S(1)}, bf16[128,1024]{1,0:T(8,128)(2,1)S(1)}, u32[]{:S(2)}, u32[]{:S(2)}) collective-permute-start(bf16[128,1024]{1,0:T(8,128)(2,1)S(1)} %get-tuple-element.159), channel_id=1, source_target_pairs={{0,4},{2,6},{4,0},{6,2},{8,12},{10,14},{12,8},{14,10},{16,20},{18,... | collective-permute-start | bytes 786440 | tf_op jit(solution)/shard_map/ppermute | solution.py:36
  336.5 36.1 %collective-permute-start.39 = (bf16[384,1024]{1,0:T(8,128)(2,1)S(1)}, bf16[384,1024]{1,0:T(8,128)(2,1)}, u32[]{:S(2)}, u32[]{:S(2)}) collective-permute-start(bf16[384,1024]{1,0:T(8,128)(2,1)S(1)} %pad_maximum_fusion.3), channel_id=1, source_target_pairs={{0,4},{2,6},{4,0},{6,2},{8,12},{10,14},{12,8},{14,10},{16,20},{18,... | collective-permute-start | bytes 2359304 | tf_op jit(solution)/shard_map/ppermute | solution.py:36
  348.7 26.7 %copy-start = (bf16[16,32,1664]{2,1,0:T(8,128)(2,1)}, bf16[16,32,1664]{2,1,0:T(8,128)(2,1)S(1)}, u32[]{:S(2)}) copy-start(bf16[16,32,1664]{2,1,0:T(8,128)(2,1)S(1)} %all-to-all-done.2.in_ref) | copy-start | bytes 5111812
  348.7 37.3 %all-to-all-start.3 = ((bf16[32,32,256]{2,1,0:T(8,128)(2,1)}), bf16[32,32,256]{2,1,0:T(8,128)(2,1)S(1)}, u32[]{:S(2)}, u32[]{:S(2)}) async-start(bf16[32,32,256]{2,1,0:T(8,128)(2,1)} %bitcast.35), calls=%async_computation.4 | async-start | bytes 1048576 | tf_op jit(solution)/shard_map/all_to_all | solution.py:1089
  375.3 26.2 %collective-permute-start.43 = (bf16[128,1024]{1,0:T(8,128)(2,1)S(1)}, bf16[128,1024]{1,0:T(8,128)(2,1)S(1)}, u32[]{:S(2)}, u32[]{:S(2)}) collective-permute-start(bf16[128,1024]{1,0:T(8,128)(2,1)S(1)} %get-tuple-element.154), channel_id=1, source_target_pairs={{0,8},{2,10},{4,12},{6,14},{8,16},{10,18},{12,20},{14,22},{16,24},... | collective-permute-start | bytes 786440 | tf_op jit(solution)/shard_map/ppermute | solution.py:36
  376.6 25.0 %collective-permute-start.42 = (bf16[128,1024]{1,0:T(8,128)(2,1)S(1)}, bf16[128,1024]{1,0:T(8,128)(2,1)S(1)}, u32[]{:S(2)}, u32[]{:S(2)}) collective-permute-start(bf16[128,1024]{1,0:T(8,128)(2,1)S(1)} %get-tuple-element.155), channel_id=1, source_target_pairs={{0,24},{2,26},{4,28},{6,30},{8,0},{10,2},{12,4},{14,6},{16,8},{18,... | collective-permute-start | bytes 786440 | tf_op jit(solution)/shard_map/ppermute | solution.py:36
  379.2 11.1 %copy-start.15 = (f32[128,1024]{1,0:T(8,128)S(1)}, f32[128,1024]{1,0:T(8,128)}, u32[]{:S(2)}) copy-start(f32[128,1024]{1,0:T(8,128)} %get-tuple-element.72) | copy-start | bytes 1572868
  379.2 22.4 %collective-permute-start.40 = (bf16[128,1024]{1,0:T(8,128)(2,1)}, bf16[128,1024]{1,0:T(8,128)(2,1)S(1)}, u32[]{:S(2)}, u32[]{:S(2)}) collective-permute-start(bf16[128,1024]{1,0:T(8,128)(2,1)} %get-tuple-element.153), channel_id=1, source_target_pairs={{0,16},{2,18},{4,20},{6,22},{8,24},{10,26},{12,28},{14,30},{16,0},... | collective-permute-start | bytes 786440 | tf_op jit(solution)/shard_map/ppermute | solution.py:36
  385.9 15.6 %copy-start.6 = (bf16[1,128,1024]{2,1,0:T(8,128)(2,1)S(1)}, bf16[1,128,1024]{2,1,0:T(8,128)(2,1)}, u32[]{:S(2)}) copy-start(bf16[1,128,1024]{2,1,0:T(8,128)(2,1)} %param.17) | copy-start | bytes 786436
  388.4 5.0 %collective-permute-start.41 = (f32[32,1024]{1,0:T(8,128)S(1)}, f32[32,1024]{1,0:T(8,128)S(1)}, u32[]{:S(2)}, u32[]{:S(2)}) collective-permute-start(f32[32,1024]{1,0:T(8,128)S(1)} %dynamic-slice_bitcast_fusion.2), channel_id=1, source_target_pairs={{0,1},{1,0},{2,3},{3,2},{4,5},{5,4},{6,7},{7,6},{8,9},{9,8},{10,11... | collective-permute-start | bytes 393224 | tf_op jit(solution)/shard_map/ppermute | solution.py:917
  (21 other events, 47.1 us)
Sparse Core Ops, SparseCore 0:
  38.6 73.8 all-gather.3
  134.6 55.6 all-gather.5
  258.5 119.9 reduce-scatter.1
